TPU v7x, 1024 devices: a whole 8x8x8 slice. The times are simulated.
1024 devices in a mesh: grp: 4 (over z_hi), gy: 16 (over y, core), gz: 16 (over z_lo, x).
Axes of the slice: x: 8, y: 8, z: 8 (z_hi: 4, z_lo: 2; z = z_hi * 2 + z_lo), core: 2. Of those that a mesh axis runs over, the one named last changes fastest.
Arguments:
- velocity: float32 [3, 128, 128, 512], P(None, 'gy', 'gz', 'grp'), may hold values from -5 to 5
- basis_old: bfloat16 [64, 3, 64, 64, 512], P(None, None, 'gy', 'gz', 'grp'), may hold values from -64 to 64
- strength: float32 [64], replicated, may hold values from 0.3 to 3
- snapshots: bfloat16 [63, 3, 64, 64, 512], P(None, None, 'gy', 'gz', 'grp'), may hold values from -64 to 64
Outputs:
- advanced: float32 [3, 128, 128, 512], P(None, 'gy', 'gz', 'grp')
- basis_new: bfloat16 [128, 3, 64, 64, 512], P(None, None, 'gy', 'gz', 'grp')
- root_factor: float32 [128, 128], replicated
All inputs are finite; a program needn't handle non-finite values.
Results may differ from a plain program's by a relative error of at most 0.0012.
The roundings to bfloat16 on the way count: a program that leaves them out, or rounds other values in their place, can miss the bound.
Values sent between devices are 32-bit elements; how exact they have to be, the bound alone decides.
No kernel may reach another device: no remote copies, remote signals or barrier semaphores. Data moves between devices by JAX's collectives and lax.ppermute only.
A program may use at most 32 MiB of HBM per device.

v0:
```python
import jax
import jax.numpy as jnp
from jax import lax
from jax.sharding import PartitionSpec as P

NS_ITERS = 8


time_step = 0.1
viscosity = 0.05


def padded_2(block, sides, width):
    for axis, dim in sides:
        count = lax.axis_size(axis)
        forward = [(i, i + 1) for i in range(count - 1)]
        forward.append((count - 1, 0))
        backward = [(target, source) for source, target in forward]
        low = lax.ppermute(
            lax.slice_in_dim(block, block.shape[dim] - width, None, axis=dim), axis, forward
        )
        high = lax.ppermute(lax.slice_in_dim(block, 0, width, axis=dim), axis, backward)
        block = jnp.concatenate([low, block, high], axis=dim)
    return block


def tendency(padded, field):
    y_plus = padded[:, 2:, 1:-1, 1:-1]
    y_minus = padded[:, :-2, 1:-1, 1:-1]
    z_plus = padded[:, 1:-1, 2:, 1:-1]
    z_minus = padded[:, 1:-1, :-2, 1:-1]
    x_plus = padded[:, 1:-1, 1:-1, 2:]
    x_minus = padded[:, 1:-1, 1:-1, :-2]
    carried = field[0][None] * (x_plus - x_minus) * 0.5
    carried = carried + field[1][None] * (y_plus - y_minus) * 0.5
    carried = carried + field[2][None] * (z_plus - z_minus) * 0.5
    spread = x_plus + x_minus + y_plus + y_minus + z_plus + z_minus - 6.0 * field
    return viscosity * spread - carried


def faces(field):
    padded = padded_2(field, (("grp", 3), ("gy", 1), ("gz", 2)), 1)
    position = lax.axis_index("gy")
    bottom = jnp.where(position == 0, 0.0, padded[:, 0, :, :])
    upper = jnp.where(position == lax.axis_size("gy") - 1, 0.0, padded[:, -1, :, :])
    return padded.at[:, 0, :, :].set(bottom).at[:, -1, :, :].set(upper)


def advance(field):
    for repeat in range(2):
        first = field + time_step * tendency(faces(field), field)
        second = 0.75 * field + 0.25 * (first + time_step * tendency(faces(first), first))
        field = field / 3.0 + 2.0 / 3.0 * (second + time_step * tendency(faces(second), second))
    return field


def local(velocity, basis_old, strength, snapshots):
    modes = basis_old.shape[0]
    earlier_count = snapshots.shape[0]
    head = (strength[:, None] * basis_old.reshape(modes, -1).astype(jnp.float32)).astype(
        jnp.bfloat16
    )
    earlier = jnp.concatenate([head, snapshots.reshape(earlier_count, -1)], axis=0)
    field = advance(velocity)
    newest = field[:, ::2, ::2, :].reshape(1, -1).astype(jnp.bfloat16)
    whole = jnp.concatenate([earlier, newest], axis=0)
    gram = lax.psum(
        jnp.dot(whole, whole.T, preferred_element_type=jnp.float32), ("grp", "gy", "gz")
    )
    ranks = whole.shape[0]
    scale = jnp.sqrt(jnp.sum(gram * gram))
    level = gram / scale
    ident = jnp.eye(ranks, dtype=jnp.float32)
    inverse = ident
    for repeat in range(NS_ITERS):
        factor = 1.5 * ident - 0.5 * jnp.dot(inverse, level, precision=lax.Precision.HIGHEST)
        level = jnp.dot(level, factor, precision=lax.Precision.HIGHEST)
        inverse = jnp.dot(factor, inverse, precision=lax.Precision.HIGHEST)
    total_rows = whole.shape[1] * lax.axis_size("grp") * lax.axis_size("gy") * lax.axis_size("gz")
    weights = (inverse * (jnp.sqrt(jnp.float32(total_rows)) / jnp.sqrt(scale))).astype(jnp.bfloat16)
    basis_new = jnp.dot(weights, whole, preferred_element_type=jnp.float32).astype(jnp.bfloat16)
    basis_new = basis_new.reshape(
        ranks, 3, field.shape[1] // 2, field.shape[2] // 2, field.shape[3]
    )
    return (field, basis_new, level)


def solution(mesh):
    placed = (
        P(None, "gy", "gz", "grp"),
        P(None, None, "gy", "gz", "grp"),
        P(),
        P(None, None, "gy", "gz", "grp"),
    )
    return jax.shard_map(
        local,
        mesh=mesh,
        in_specs=placed,
        out_specs=(P(None, "gy", "gz", "grp"), P(None, None, "gy", "gz", "grp"), P()),
        check_vma=False,
    )
```

profile of v0, /device:TPU:1, one launch (start us, length us, event | category | flops | bytes accessed | tf_op | source)
XLA Modules:
  0.0 489.5 jit_solution(18034936927156032114)
XLA Ops:
  8.3 8.6 %collective-permute-start = (f32[3,8,8,1]{3,2,1,0:T(8,128)S(1)}, f32[3,8,8,1]{3,2,1,0:T(8,128)S(1)}, u32[]{:S(2)}, u32[]{:S(2)}) collective-permute-start(f32[3,8,8,1]{3,2,1,0:T(8,128)S(1)} %get-tuple-element.201), channel_id=1, source_target_pairs={{0,256},{256,512},{512,768},{768,0},{1,257},{257,513},{513,769},{7... | collective-permute-start | bytes 2312 | tf_op jit(solution)/shard_map/ppermute | solution.py:19
  16.9 10.4 %collective-permute-start.1 = (f32[3,8,8,1]{3,2,1,0:T(8,128)S(1)}, f32[3,8,8,1]{3,2,1,0:T(8,128)S(1)}, u32[]{:S(2)}, u32[]{:S(2)}) collective-permute-start(f32[3,8,8,1]{3,2,1,0:T(8,128)S(1)} %get-tuple-element.202), channel_id=1, source_target_pairs={{256,0},{512,256},{768,512},{0,768},{257,1},{513,257},{769,513},{1... | collective-permute-start | bytes 2312 | tf_op jit(solution)/shard_map/ppermute | solution.py:22
  27.4 1.5 collective-permute-done.1
  29.7 3.9 collective-permute-start.2
  33.6 1.5 collective-permute-start.3
  36.8 1.2 pad_maximum_fusion.38
  38.0 3.1 collective-permute-start.4
  41.2 5.0 %collective-permute-start.5 = (f32[3,10,1,130]{3,2,1,0:T(1,128)S(1)}, f32[3,10,1,130]{3,2,1,0:T(1,128)S(1)}, u32[]{:S(2)}, u32[]{:S(2)}) collective-permute-start(f32[3,10,1,130]{3,2,1,0:T(1,128)S(1)} %get-tuple-element.160), channel_id=1, source_target_pairs={{1,0},{2,1},{3,2},{4,3},{5,4},{6,5},{7,6},{8,7},{9,8},{10,9},{11,1... | collective-permute-start | bytes 46808 | tf_op jit(solution)/shard_map/ppermute | solution.py:22
  48.7 6.2 %collective-permute-start.6 = (f32[3,8,8,1]{3,2,1,0:T(8,128)S(1)}, f32[3,8,8,1]{3,2,1,0:T(8,128)S(1)}, u32[]{:S(2)}, u32[]{:S(2)}) collective-permute-start(f32[3,8,8,1]{3,2,1,0:T(8,128)S(1)} %get-tuple-element.196), channel_id=1, source_target_pairs={{0,256},{256,512},{512,768},{768,0},{1,257},{257,513},{513,769},{7... | collective-permute-start | bytes 2312 | tf_op jit(solution)/shard_map/ppermute | solution.py:19
  54.9 2.2 collective-permute-start.7
  57.2 4.2 collective-permute-done.7
  61.6 3.9 collective-permute-start.8
  66.4 2.3 collective-permute-done.9
  69.0 1.9 collective-permute-start.10
  70.9 5.5 %collective-permute-start.11 = (f32[3,10,1,130]{3,2,1,0:T(1,128)S(1)}, f32[3,10,1,130]{3,2,1,0:T(1,128)S(1)}, u32[]{:S(2)}, u32[]{:S(2)}) collective-permute-start(f32[3,10,1,130]{3,2,1,0:T(1,128)S(1)} %get-tuple-element.158), channel_id=1, source_target_pairs={{1,0},{2,1},{3,2},{4,3},{5,4},{6,5},{7,6},{8,7},{9,8},{10,9},{11,1... | collective-permute-start | bytes 46808 | tf_op jit(solution)/shard_map/ppermute | solution.py:22
  78.0 4.6 collective-permute-start.12
  82.6 2.8 collective-permute-start.13
  86.0 2.8 collective-permute-done.13
  88.9 2.8 collective-permute-start.14
  91.8 2.4 collective-permute-start.15
  95.3 2.8 collective-permute-start.16
  98.1 5.0 %collective-permute-start.17 = (f32[3,10,1,130]{3,2,1,0:T(1,128)S(1)}, f32[3,10,1,130]{3,2,1,0:T(1,128)S(1)}, u32[]{:S(2)}, u32[]{:S(2)}) collective-permute-start(f32[3,10,1,130]{3,2,1,0:T(1,128)S(1)} %get-tuple-element.156), channel_id=1, source_target_pairs={{1,0},{2,1},{3,2},{4,3},{5,4},{6,5},{7,6},{8,7},{9,8},{10,9},{11,1... | collective-permute-start | bytes 46808 | tf_op jit(solution)/shard_map/ppermute | solution.py:22
  104.6 6.1 %collective-permute-start.18 = (f32[3,8,8,1]{3,2,1,0:T(8,128)S(1)}, f32[3,8,8,1]{3,2,1,0:T(8,128)S(1)}, u32[]{:S(2)}, u32[]{:S(2)}) collective-permute-start(f32[3,8,8,1]{3,2,1,0:T(8,128)S(1)} %get-tuple-element.186), channel_id=1, source_target_pairs={{0,256},{256,512},{512,768},{768,0},{1,257},{257,513},{513,769},{7... | collective-permute-start | bytes 2312 | tf_op jit(solution)/shard_map/ppermute | solution.py:19
  110.8 1.9 collective-permute-start.19
  112.7 4.6 collective-permute-done.19
  117.4 5.1 %collective-permute-start.20 = (f32[3,1,8,130]{3,2,1,0:T(8,128)S(1)}, f32[3,1,8,130]{3,2,1,0:T(8,128)S(1)}, u32[]{:S(2)}, u32[]{:S(2)}) collective-permute-start(f32[3,1,8,130]{3,2,1,0:T(8,128)S(1)} %get-tuple-element.165), channel_id=1, source_target_pairs={{0,16},{16,32},{32,48},{48,64},{64,80},{80,96},{96,112},{112,128},... | collective-permute-start | bytes 37448 | tf_op jit(solution)/shard_map/ppermute | solution.py:19
  123.5 2.5 collective-permute-done.21
  126.2 3.1 collective-permute-start.22
  129.3 4.5 collective-permute-start.23
  135.4 3.6 collective-permute-start.24
  139.0 3.8 collective-permute-start.25
  142.9 2.6 collective-permute-done.25
  145.6 3.8 collective-permute-start.26
  150.4 2.5 collective-permute-done.27
  153.1 2.5 collective-permute-start.28
  155.6 4.9 %collective-permute-start.29 = (f32[3,10,1,130]{3,2,1,0:T(1,128)S(1)}, f32[3,10,1,130]{3,2,1,0:T(1,128)S(1)}, u32[]{:S(2)}, u32[]{:S(2)}) collective-permute-start(f32[3,10,1,130]{3,2,1,0:T(1,128)S(1)} %get-tuple-element.152), channel_id=1, source_target_pairs={{1,0},{2,1},{3,2},{4,3},{5,4},{6,5},{7,6},{8,7},{9,8},{10,9},{11,1... | collective-permute-start | bytes 46808 | tf_op jit(solution)/shard_map/ppermute | solution.py:22
  162.1 2.0 collective-permute-start.30
  164.2 5.4 %collective-permute-start.31 = (f32[3,8,8,1]{3,2,1,0:T(8,128)S(1)}, f32[3,8,8,1]{3,2,1,0:T(8,128)S(1)}, u32[]{:S(2)}, u32[]{:S(2)}) collective-permute-start(f32[3,8,8,1]{3,2,1,0:T(8,128)S(1)} %get-tuple-element.174), channel_id=1, source_target_pairs={{256,0},{512,256},{768,512},{0,768},{257,1},{513,257},{769,513},{1... | collective-permute-start | bytes 2312 | tf_op jit(solution)/shard_map/ppermute | solution.py:22
  170.0 1.2 collective-permute-done.31
  171.9 4.4 collective-permute-start.32
  176.2 1.6 collective-permute-start.33
  178.0 1.7 reshape.418
  180.8 4.8 collective-permute-start.34
  185.6 4.3 collective-permute-start.35
  193.0 1.2 fusion.9
  194.2 276.4 %all-reduce.2.cloned.1.call-done = f32[128,128]{1,0:T(8,128)} async-done(((f32[128,128]{1,0:T(8,128)}), f32[128,128]{1,0:T(8,128)}) %all-reduce.2.cloned.1.call-update) | async-done | bytes 65552 | tf_op jit(solution)/shard_map/psum | solution.py:67
  470.5 1.5 multiply_reduce_fusion
  480.7 2.0 reshape.419
  (120 shorter events, 31.2 us)
Async XLA Ops:
  7.2 463.4 %all-reduce.2.cloned.1.call-start = ((), (), s32[]{:S(2)}) async-start(), calls=%async_computation | async-start | bytes 131072 | tf_op jit(solution)/shard_map/psum | solution.py:67
  8.3 40.1 %copy-start = (f32[3,8,8,128]{3,2,1,0:T(8,128)S(1)}, f32[3,8,8,128]{3,2,1,0:T(8,128)}, u32[]{:S(2)}) copy-start(f32[3,8,8,128]{3,2,1,0:T(8,128)} %param.28) | copy-start | bytes 294916
  8.3 19.1 %collective-permute-start = (f32[3,8,8,1]{3,2,1,0:T(8,128)S(1)}, f32[3,8,8,1]{3,2,1,0:T(8,128)S(1)}, u32[]{:S(2)}, u32[]{:S(2)}) collective-permute-start(f32[3,8,8,1]{3,2,1,0:T(8,128)S(1)} %get-tuple-element.201), channel_id=1, source_target_pairs={{0,256},{256,512},{512,768},{768,0},{1,257},{257,513},{513,769},{7... | collective-permute-start | bytes 2312 | tf_op jit(solution)/shard_map/ppermute | solution.py:19
  16.9 12.0 %collective-permute-start.1 = (f32[3,8,8,1]{3,2,1,0:T(8,128)S(1)}, f32[3,8,8,1]{3,2,1,0:T(8,128)S(1)}, u32[]{:S(2)}, u32[]{:S(2)}) collective-permute-start(f32[3,8,8,1]{3,2,1,0:T(8,128)S(1)} %get-tuple-element.202), channel_id=1, source_target_pairs={{256,0},{512,256},{768,512},{0,768},{257,1},{513,257},{769,513},{1... | collective-permute-start | bytes 2312 | tf_op jit(solution)/shard_map/ppermute | solution.py:22
  29.7 6.0 %collective-permute-start.2 = (f32[3,1,8,130]{3,2,1,0:T(8,128)S(1)}, f32[3,1,8,130]{3,2,1,0:T(8,128)S(1)}, u32[]{:S(2)}, u32[]{:S(2)}) collective-permute-start(f32[3,1,8,130]{3,2,1,0:T(8,128)S(1)} %get-tuple-element.171), channel_id=1, source_target_pairs={{0,16},{16,32},{32,48},{48,64},{64,80},{80,96},{96,112},{112,128},... | collective-permute-start | bytes 37448 | tf_op jit(solution)/shard_map/ppermute | solution.py:19
  33.6 3.3 collective-permute-start.3
  38.0 9.0 %collective-permute-start.4 = (f32[3,10,1,130]{3,2,1,0:T(1,128)S(1)}, f32[3,10,1,130]{3,2,1,0:T(1,128)S(1)}, u32[]{:S(2)}, u32[]{:S(2)}) collective-permute-start(f32[3,10,1,130]{3,2,1,0:T(1,128)S(1)} %get-tuple-element.159), channel_id=1, source_target_pairs={{0,1},{1,2},{2,3},{3,4},{4,5},{5,6},{6,7},{7,8},{8,9},{9,10},{10,1... | collective-permute-start | bytes 46808 | tf_op jit(solution)/shard_map/ppermute | solution.py:19
  41.2 6.0 %collective-permute-start.5 = (f32[3,10,1,130]{3,2,1,0:T(1,128)S(1)}, f32[3,10,1,130]{3,2,1,0:T(1,128)S(1)}, u32[]{:S(2)}, u32[]{:S(2)}) collective-permute-start(f32[3,10,1,130]{3,2,1,0:T(1,128)S(1)} %get-tuple-element.160), channel_id=1, source_target_pairs={{1,0},{2,1},{3,2},{4,3},{5,4},{6,5},{7,6},{8,7},{9,8},{10,9},{11,1... | collective-permute-start | bytes 46808 | tf_op jit(solution)/shard_map/ppermute | solution.py:22
  48.7 8.6 %collective-permute-start.6 = (f32[3,8,8,1]{3,2,1,0:T(8,128)S(1)}, f32[3,8,8,1]{3,2,1,0:T(8,128)S(1)}, u32[]{:S(2)}, u32[]{:S(2)}) collective-permute-start(f32[3,8,8,1]{3,2,1,0:T(8,128)S(1)} %get-tuple-element.196), channel_id=1, source_target_pairs={{0,256},{256,512},{512,768},{768,0},{1,257},{257,513},{513,769},{7... | collective-permute-start | bytes 2312 | tf_op jit(solution)/shard_map/ppermute | solution.py:19
  54.9 6.6 %collective-permute-start.7 = (f32[3,8,8,1]{3,2,1,0:T(8,128)S(1)}, f32[3,8,8,1]{3,2,1,0:T(8,128)S(1)}, u32[]{:S(2)}, u32[]{:S(2)}) collective-permute-start(f32[3,8,8,1]{3,2,1,0:T(8,128)S(1)} %get-tuple-element.197), channel_id=1, source_target_pairs={{256,0},{512,256},{768,512},{0,768},{257,1},{513,257},{769,513},{1... | collective-permute-start | bytes 2312 | tf_op jit(solution)/shard_map/ppermute | solution.py:22
  61.6 4.9 collective-permute-start.8
  65.5 3.3 collective-permute-start.9
  69.0 7.4 %collective-permute-start.10 = (f32[3,10,1,130]{3,2,1,0:T(1,128)S(1)}, f32[3,10,1,130]{3,2,1,0:T(1,128)S(1)}, u32[]{:S(2)}, u32[]{:S(2)}) collective-permute-start(f32[3,10,1,130]{3,2,1,0:T(1,128)S(1)} %get-tuple-element.157), channel_id=1, source_target_pairs={{0,1},{1,2},{2,3},{3,4},{4,5},{5,6},{6,7},{7,8},{8,9},{9,10},{10,1... | collective-permute-start | bytes 46808 | tf_op jit(solution)/shard_map/ppermute | solution.py:19
  70.9 6.5 %collective-permute-start.11 = (f32[3,10,1,130]{3,2,1,0:T(1,128)S(1)}, f32[3,10,1,130]{3,2,1,0:T(1,128)S(1)}, u32[]{:S(2)}, u32[]{:S(2)}) collective-permute-start(f32[3,10,1,130]{3,2,1,0:T(1,128)S(1)} %get-tuple-element.158), channel_id=1, source_target_pairs={{1,0},{2,1},{3,2},{4,3},{5,4},{6,5},{7,6},{8,7},{9,8},{10,9},{11,1... | collective-permute-start | bytes 46808 | tf_op jit(solution)/shard_map/ppermute | solution.py:22
  78.0 8.1 %collective-permute-start.12 = (f32[3,8,8,1]{3,2,1,0:T(8,128)S(1)}, f32[3,8,8,1]{3,2,1,0:T(8,128)S(1)}, u32[]{:S(2)}, u32[]{:S(2)}) collective-permute-start(f32[3,8,8,1]{3,2,1,0:T(8,128)S(1)} %get-tuple-element.191), channel_id=1, source_target_pairs={{0,256},{256,512},{512,768},{768,0},{1,257},{257,513},{513,769},{7... | collective-permute-start | bytes 2312 | tf_op jit(solution)/shard_map/ppermute | solution.py:19
  82.6 6.3 %collective-permute-start.13 = (f32[3,8,8,1]{3,2,1,0:T(8,128)S(1)}, f32[3,8,8,1]{3,2,1,0:T(8,128)S(1)}, u32[]{:S(2)}, u32[]{:S(2)}) collective-permute-start(f32[3,8,8,1]{3,2,1,0:T(8,128)S(1)} %get-tuple-element.192), channel_id=1, source_target_pairs={{256,0},{512,256},{768,512},{0,768},{257,1},{513,257},{769,513},{1... | collective-permute-start | bytes 2312 | tf_op jit(solution)/shard_map/ppermute | solution.py:22
  88.9 5.9 %collective-permute-start.14 = (f32[3,1,8,130]{3,2,1,0:T(8,128)S(1)}, f32[3,1,8,130]{3,2,1,0:T(8,128)S(1)}, u32[]{:S(2)}, u32[]{:S(2)}) collective-permute-start(f32[3,1,8,130]{3,2,1,0:T(8,128)S(1)} %get-tuple-element.167), channel_id=1, source_target_pairs={{0,16},{16,32},{32,48},{48,64},{64,80},{80,96},{96,112},{112,128},... | collective-permute-start | bytes 37448 | tf_op jit(solution)/shard_map/ppermute | solution.py:19
  91.8 3.3 collective-permute-start.15
  95.3 7.8 %collective-permute-start.16 = (f32[3,10,1,130]{3,2,1,0:T(1,128)S(1)}, f32[3,10,1,130]{3,2,1,0:T(1,128)S(1)}, u32[]{:S(2)}, u32[]{:S(2)}) collective-permute-start(f32[3,10,1,130]{3,2,1,0:T(1,128)S(1)} %get-tuple-element.155), channel_id=1, source_target_pairs={{0,1},{1,2},{2,3},{3,4},{4,5},{5,6},{6,7},{7,8},{8,9},{9,10},{10,1... | collective-permute-start | bytes 46808 | tf_op jit(solution)/shard_map/ppermute | solution.py:19
  98.1 6.0 %collective-permute-start.17 = (f32[3,10,1,130]{3,2,1,0:T(1,128)S(1)}, f32[3,10,1,130]{3,2,1,0:T(1,128)S(1)}, u32[]{:S(2)}, u32[]{:S(2)}) collective-permute-start(f32[3,10,1,130]{3,2,1,0:T(1,128)S(1)} %get-tuple-element.156), channel_id=1, source_target_pairs={{1,0},{2,1},{3,2},{4,3},{5,4},{6,5},{7,6},{8,7},{9,8},{10,9},{11,1... | collective-permute-start | bytes 46808 | tf_op jit(solution)/shard_map/ppermute | solution.py:22
  104.6 8.0 %collective-permute-start.18 = (f32[3,8,8,1]{3,2,1,0:T(8,128)S(1)}, f32[3,8,8,1]{3,2,1,0:T(8,128)S(1)}, u32[]{:S(2)}, u32[]{:S(2)}) collective-permute-start(f32[3,8,8,1]{3,2,1,0:T(8,128)S(1)} %get-tuple-element.186), channel_id=1, source_target_pairs={{0,256},{256,512},{512,768},{768,0},{1,257},{257,513},{513,769},{7... | collective-permute-start | bytes 2312 | tf_op jit(solution)/shard_map/ppermute | solution.py:19
  110.8 6.6 %collective-permute-start.19 = (f32[3,8,8,1]{3,2,1,0:T(8,128)S(1)}, f32[3,8,8,1]{3,2,1,0:T(8,128)S(1)}, u32[]{:S(2)}, u32[]{:S(2)}) collective-permute-start(f32[3,8,8,1]{3,2,1,0:T(8,128)S(1)} %get-tuple-element.187), channel_id=1, source_target_pairs={{256,0},{512,256},{768,512},{0,768},{257,1},{513,257},{769,513},{1... | collective-permute-start | bytes 2312 | tf_op jit(solution)/shard_map/ppermute | solution.py:22
  117.4 6.1 %collective-permute-start.20 = (f32[3,1,8,130]{3,2,1,0:T(8,128)S(1)}, f32[3,1,8,130]{3,2,1,0:T(8,128)S(1)}, u32[]{:S(2)}, u32[]{:S(2)}) collective-permute-start(f32[3,1,8,130]{3,2,1,0:T(8,128)S(1)} %get-tuple-element.165), channel_id=1, source_target_pairs={{0,16},{16,32},{32,48},{48,64},{64,80},{80,96},{96,112},{112,128},... | collective-permute-start | bytes 37448 | tf_op jit(solution)/shard_map/ppermute | solution.py:19
  122.5 3.4 collective-permute-start.21
  126.2 7.6 %collective-permute-start.22 = (f32[3,10,1,130]{3,2,1,0:T(1,128)S(1)}, f32[3,10,1,130]{3,2,1,0:T(1,128)S(1)}, u32[]{:S(2)}, u32[]{:S(2)}) collective-permute-start(f32[3,10,1,130]{3,2,1,0:T(1,128)S(1)} %get-tuple-element.153), channel_id=1, source_target_pairs={{0,1},{1,2},{2,3},{3,4},{4,5},{5,6},{6,7},{7,8},{8,9},{9,10},{10,1... | collective-permute-start | bytes 46808 | tf_op jit(solution)/shard_map/ppermute | solution.py:19
  129.3 5.4 %collective-permute-start.23 = (f32[3,10,1,130]{3,2,1,0:T(1,128)S(1)}, f32[3,10,1,130]{3,2,1,0:T(1,128)S(1)}, u32[]{:S(2)}, u32[]{:S(2)}) collective-permute-start(f32[3,10,1,130]{3,2,1,0:T(1,128)S(1)} %get-tuple-element.154), channel_id=1, source_target_pairs={{1,0},{2,1},{3,2},{4,3},{5,4},{6,5},{7,6},{8,7},{9,8},{10,9},{11,1... | collective-permute-start | bytes 46808 | tf_op jit(solution)/shard_map/ppermute | solution.py:22
  135.4 7.6 %collective-permute-start.24 = (f32[3,8,8,1]{3,2,1,0:T(8,128)S(1)}, f32[3,8,8,1]{3,2,1,0:T(8,128)S(1)}, u32[]{:S(2)}, u32[]{:S(2)}) collective-permute-start(f32[3,8,8,1]{3,2,1,0:T(8,128)S(1)} %get-tuple-element.181), channel_id=1, source_target_pairs={{0,256},{256,512},{512,768},{768,0},{1,257},{257,513},{513,769},{7... | collective-permute-start | bytes 2312 | tf_op jit(solution)/shard_map/ppermute | solution.py:19
  139.0 6.6 %collective-permute-start.25 = (f32[3,8,8,1]{3,2,1,0:T(8,128)S(1)}, f32[3,8,8,1]{3,2,1,0:T(8,128)S(1)}, u32[]{:S(2)}, u32[]{:S(2)}) collective-permute-start(f32[3,8,8,1]{3,2,1,0:T(8,128)S(1)} %get-tuple-element.182), channel_id=1, source_target_pairs={{256,0},{512,256},{768,512},{0,768},{257,1},{513,257},{769,513},{1... | collective-permute-start | bytes 2312 | tf_op jit(solution)/shard_map/ppermute | solution.py:22
  145.6 4.8 collective-permute-start.26
  149.5 3.4 collective-permute-start.27
  153.1 7.4 %collective-permute-start.28 = (f32[3,10,1,130]{3,2,1,0:T(1,128)S(1)}, f32[3,10,1,130]{3,2,1,0:T(1,128)S(1)}, u32[]{:S(2)}, u32[]{:S(2)}) collective-permute-start(f32[3,10,1,130]{3,2,1,0:T(1,128)S(1)} %get-tuple-element.151), channel_id=1, source_target_pairs={{0,1},{1,2},{2,3},{3,4},{4,5},{5,6},{6,7},{7,8},{8,9},{9,10},{10,1... | collective-permute-start | bytes 46808 | tf_op jit(solution)/shard_map/ppermute | solution.py:19
  155.6 5.9 %collective-permute-start.29 = (f32[3,10,1,130]{3,2,1,0:T(1,128)S(1)}, f32[3,10,1,130]{3,2,1,0:T(1,128)S(1)}, u32[]{:S(2)}, u32[]{:S(2)}) collective-permute-start(f32[3,10,1,130]{3,2,1,0:T(1,128)S(1)} %get-tuple-element.152), channel_id=1, source_target_pairs={{1,0},{2,1},{3,2},{4,3},{5,4},{6,5},{7,6},{8,7},{9,8},{10,9},{11,1... | collective-permute-start | bytes 46808 | tf_op jit(solution)/shard_map/ppermute | solution.py:22
  160.6 9.0 %copy-start.1 = (bf16[64,3,4,4,128]{4,3,2,1,0:T(4,128)(2,1)S(1)}, bf16[64,3,4,4,128]{4,3,2,1,0:T(4,128)(2,1)}, u32[]{:S(2)}) copy-start(bf16[64,3,4,4,128]{4,3,2,1,0:T(4,128)(2,1)} %param.29) | copy-start | bytes 2359300
  162.0 15.8 %copy-start.2 = (f32[64]{0:T(128)S(1)}, f32[64]{0:T(128)}, u32[]{:S(2)}) copy-start(f32[64]{0:T(128)} %param.30) | copy-start | bytes 772
  162.1 7.8 %collective-permute-start.30 = (f32[3,8,8,1]{3,2,1,0:T(8,128)S(1)}, f32[3,8,8,1]{3,2,1,0:T(8,128)S(1)}, u32[]{:S(2)}, u32[]{:S(2)}) collective-permute-start(f32[3,8,8,1]{3,2,1,0:T(8,128)S(1)} %get-tuple-element.173), channel_id=1, source_target_pairs={{0,256},{256,512},{512,768},{768,0},{1,257},{257,513},{513,769},{7... | collective-permute-start | bytes 2312 | tf_op jit(solution)/shard_map/ppermute | solution.py:19
  164.2 7.0 %collective-permute-start.31 = (f32[3,8,8,1]{3,2,1,0:T(8,128)S(1)}, f32[3,8,8,1]{3,2,1,0:T(8,128)S(1)}, u32[]{:S(2)}, u32[]{:S(2)}) collective-permute-start(f32[3,8,8,1]{3,2,1,0:T(8,128)S(1)} %get-tuple-element.174), channel_id=1, source_target_pairs={{256,0},{512,256},{768,512},{0,768},{257,1},{513,257},{769,513},{1... | collective-permute-start | bytes 2312 | tf_op jit(solution)/shard_map/ppermute | solution.py:22
  171.9 7.9 %collective-permute-start.32 = (f32[3,1,8,130]{3,2,1,0:T(8,128)}, f32[3,1,8,130]{3,2,1,0:T(8,128)}, u32[]{:S(2)}, u32[]{:S(2)}) collective-permute-start(f32[3,1,8,130]{3,2,1,0:T(8,128)} %get-tuple-element.161), channel_id=1, source_target_pairs={{0,16},{16,32},{32,48},{48,64},{64,80},{80,96},{96,112},{112,128},... | collective-permute-start | bytes 37448 | tf_op jit(solution)/shard_map/ppermute | solution.py:19
  176.2 3.6 collective-permute-start.33
  180.8 9.1 %collective-permute-start.34 = (f32[3,10,1,130]{3,2,1,0:T(1,128)S(1)}, f32[3,10,1,130]{3,2,1,0:T(1,128)S(1)}, u32[]{:S(2)}, u32[]{:S(2)}) collective-permute-start(f32[3,10,1,130]{3,2,1,0:T(1,128)S(1)} %get-tuple-element.149), channel_id=1, source_target_pairs={{0,1},{1,2},{2,3},{3,4},{4,5},{5,6},{6,7},{7,8},{8,9},{9,10},{10,1... | collective-permute-start | bytes 46808 | tf_op jit(solution)/shard_map/ppermute | solution.py:19
  185.6 5.1 %collective-permute-start.35 = (f32[3,10,1,130]{3,2,1,0:T(1,128)S(1)}, f32[3,10,1,130]{3,2,1,0:T(1,128)S(1)}, u32[]{:S(2)}, u32[]{:S(2)}) collective-permute-start(f32[3,10,1,130]{3,2,1,0:T(1,128)S(1)} %get-tuple-element.150), channel_id=1, source_target_pairs={{1,0},{2,1},{3,2},{4,3},{5,4},{6,5},{7,6},{8,7},{9,8},{10,9},{11,1... | collective-permute-start | bytes 46808 | tf_op jit(solution)/shard_map/ppermute | solution.py:22
Sparse Core Ops, SparseCore 0:
  194.3 276.1 all-reduce.1
where the time goes:
time: 491 us; the launch traced here: 490 us
  waiting for transfers between devices  312 us (64%)
  starting transfers between devices  134 us (27%)
  between operations  15.6 us (3%)
  other arithmetic  11.5 us (2%)
  matrix products  8.93 us (2%)
  local copies, waits for them, and re-layouts  7.02 us (1%)
    psum x1, waiting for transfers between devices, local(): lax.psum(jnp.dot(whole, whole.T, preferred_element_type=jnp.float32), ('g...  276 us
    ppermute x18, starting transfers between devices, padded_2(): lax.ppermute(lax.slice_in_dim(block, block.shape[dim] - width, None, axis...  73.3 us
    ppermute x18, starting transfers between devices, padded_2(): lax.ppermute(lax.slice_in_dim(block, 0, width, axis=dim), axis, backward)  61.1 us
    ppermute x18, waiting for transfers between devices, padded_2(): lax.ppermute(lax.slice_in_dim(block, 0, width, axis=dim), axis, backward)  30.4 us
  transfers between devices with their start and end apart: 37, of which 28 were waited for; matrix products, arithmetic and copies ran while one was open for 1% of the time, Pallas kernels for 0%

commit v1 on v0

v1 whole, which is shorter than its diff:
```python
import functools
import jax
import jax.numpy as jnp
from jax import lax
from jax.experimental import pallas as pl
from jax.experimental.pallas import tpu as pltpu
from jax.sharding import PartitionSpec as P

NS_ITERS = 8

HALO = 6
PLANES = 20
DT = 0.1
VISC = 0.05


def _lanes():
    return lax.broadcasted_iota(jnp.int32, (8, 128), 1)


def _faces_y_kernel(v_ref, zl_ref, zh_ref, low_ref, high_ref):
    for part, source in enumerate((zl_ref, v_ref, zh_ref)):
        rows = pl.ds(8 * part, 8)
        low_ref[:, :, rows, :] = source[:, 0:HALO]
        high_ref[:, :, rows, :] = source[:, 8 - HALO : 8]


def _plane(part, c, k, v_refs, yl_ref, yh_ref):
    rows = pl.ds(8 * part, 8)
    if k < HALO:
        return yl_ref[c, k, rows, :]
    if k < HALO + 8:
        return v_refs[part][c, k - HALO]
    return yh_ref[c, k - HALO - 8, rows, :]


def _faces_x_kernel(v_ref, zl_ref, zh_ref, yl_ref, yh_ref, low_ref, high_ref):
    lane = _lanes()
    sources = (zl_ref, v_ref, zh_ref)
    for c in range(3):
        for part in range(3):
            low = high = None
            for k in range(PLANES):
                tile = _plane(part, c, k, sources, yl_ref, yh_ref)
                first = pltpu.roll(tile, (HALO * k) % 128, 1)
                last = pltpu.roll(tile, (HALO * k + HALO) % 128, 1)
                if k == 0:
                    low, high = first, last
                else:
                    keep = lane < HALO * k
                    low = jnp.where(keep, low, first)
                    high = jnp.where(keep, high, last)
            low_ref[3 * c + part] = low
            high_ref[3 * c + part] = high


def _rotated(tiles, lane):
    up = [pltpu.roll(t, 127, 1) for t in tiles]
    down = [pltpu.roll(t, 1, 1) for t in tiles]
    plus = [jnp.where(lane == 127, up[1 - i], up[i]) for i in range(2)]
    minus = [jnp.where(lane == 0, down[1 - i], down[i]) for i in range(2)]
    return plus, minus


def _euler(u_ref, y, row, tiles):
    lane = _lanes()
    u = [[u_ref[c, y, t, row : row + 8, :] for t in range(2)] for c in range(3)]
    half = [[u[c][t] * (0.5 * DT) for t in range(tiles)] for c in range(3)]
    out = []
    for c in range(3):
        plus, minus = _rotated(u[c], lane)
        outs = []
        for t in range(tiles):
            yp = u_ref[c, y + 1, t, row : row + 8, :]
            ym = u_ref[c, y - 1, t, row : row + 8, :]
            zp = u_ref[c, y, t, row + 1 : row + 9, :]
            zm = u_ref[c, y, t, row - 1 : row + 7, :]
            carried = (
                half[0][t] * (plus[t] - minus[t])
                + half[1][t] * (yp - ym)
                + half[2][t] * (zp - zm)
            )
            around = (plus[t] + minus[t]) + (yp + ym) + (zp + zm)
            outs.append(u[c][t] + ((DT * VISC) * (around - 6.0 * u[c][t]) - carried))
        out.append(outs)
    return out


def _stencil_kernel(
    gy_ref, v_ref, zl_ref, zh_ref, yl_ref, yh_ref, xh_ref, xl_ref, adv_ref, new_ref, a_ref, b_ref, c_ref, *, last
):
    lane = _lanes()
    sources = (zl_ref, v_ref, zh_ref)
    for part in range(3):
        rows = pl.ds(8 + 8 * part, 8)
        a_ref[:, HALO : HALO + 8, 0, rows, :] = sources[part][...]
        a_ref[:, 0:HALO, 0, rows, :] = yl_ref[:, :, pl.ds(8 * part, 8), :]
        a_ref[:, HALO + 8 : PLANES, 0, rows, :] = yh_ref[:, :, pl.ds(8 * part, 8), :]
        for c in range(3):
            right = xh_ref[3 * c + part]
            left = xl_ref[3 * c + part]
            for k in range(PLANES):
                a_ref[c, k, 1, rows, :] = jnp.where(
                    lane < 64,
                    pltpu.roll(right, (-HALO * k) % 128, 1),
                    pltpu.roll(left, (128 - HALO - HALO * k) % 128, 1),
                )

    gy = gy_ref[0]

    def close(ref):
        @pl.when(gy == 0)
        def _():
            ref[:, HALO - 1] = jnp.zeros((3, 2, 40, 128), jnp.float32)

        @pl.when(gy == last)
        def _():
            ref[:, HALO + 8] = jnp.zeros((3, 2, 40, 128), jnp.float32)

    def stage(source, target, combine, depth):
        @pl.loop(depth, PLANES - depth)
        def _(y):
            for row in (8, 16, 24):
                moved = _euler(source, y, row, 2)
                for c in range(3):
                    for t in range(2):
                        target[c, y, t, row : row + 8, :] = combine(moved[c][t], c, y, t, row)

        close(target)

    def keep(w, c, y, t, row):
        return w

    def quarter(w, c, y, t, row):
        return 0.75 * a_ref[c, y, t, row : row + 8, :] + 0.25 * w

    def third(w, c, y, t, row):
        return a_ref[c, y, t, row : row + 8, :] * (1.0 / 3.0) + (2.0 / 3.0) * w

    close(a_ref)
    stage(a_ref, b_ref, keep, 1)
    stage(b_ref, c_ref, quarter, 2)
    stage(c_ref, a_ref, third, 3)
    stage(a_ref, b_ref, keep, 4)
    stage(b_ref, c_ref, quarter, 5)
    for y in range(HALO, HALO + 8):
        moved = _euler(c_ref, y, 16, 1)
        for c in range(3):
            adv_ref[c, y - HALO] = third(moved[c][0], c, y, 0, 16)
    for c in range(3):
        for y in range(0, 8, 2):
            new_ref[c, y // 2] = adv_ref[c, y, pl.ds(0, 4, stride=2), :]


VMEM_SPEC = pl.BlockSpec(memory_space=pltpu.VMEM)
SMEM_SPEC = pl.BlockSpec(memory_space=pltpu.SMEM)


def shift(x, axis, step):
    n = lax.axis_size(axis)
    return lax.ppermute(x, axis, [(i, (i + step) % n) for i in range(n)])


def advance(v):
    f32 = jnp.float32
    zl = shift(v, "gz", 1)
    zh = shift(v, "gz", -1)
    low, high = pl.pallas_call(
        _faces_y_kernel,
        out_shape=[jax.ShapeDtypeStruct((3, HALO, 24, 128), f32)] * 2,
        in_specs=[VMEM_SPEC] * 3,
        out_specs=[VMEM_SPEC] * 2,
        name="faces_y",
    )(v, zl, zh)
    yl = shift(high, "gy", 1)
    yh = shift(low, "gy", -1)
    low, high = pl.pallas_call(
        _faces_x_kernel,
        out_shape=[jax.ShapeDtypeStruct((9, 8, 128), f32)] * 2,
        in_specs=[VMEM_SPEC] * 5,
        out_specs=[VMEM_SPEC] * 2,
        name="faces_x",
    )(v, zl, zh, yl, yh)
    xl = shift(high, "grp", 1)
    xh = shift(low, "grp", -1)
    gy = lax.axis_index("gy").astype(jnp.int32).reshape(1)
    return pl.pallas_call(
        functools.partial(_stencil_kernel, last=lax.axis_size("gy") - 1),
        out_shape=[jax.ShapeDtypeStruct((3, 8, 8, 128), f32), jax.ShapeDtypeStruct((3, 4, 4, 128), f32)],
        in_specs=[SMEM_SPEC] + [VMEM_SPEC] * 7,
        out_specs=[VMEM_SPEC] * 2,
        scratch_shapes=[pltpu.VMEM((3, PLANES, 2, 40, 128), f32)] * 3,
        name="stencil",
    )(gy, v, zl, zh, yl, yh, xh, xl)


def _pack_kernel(g_ref, out_ref):
    row = lax.broadcasted_iota(jnp.int32, (64, 128), 0)
    lane = lax.broadcasted_iota(jnp.int32, (64, 128), 1)
    top = g_ref[0:64, :]
    bottom = g_ref[64:128, :]
    out_ref[0:64, :] = jnp.where(lane < row, pltpu.roll(bottom, 64, 1), top)
    diagonal = jnp.where(lane == row + 64, bottom, 0.0)
    out_ref[64:72, :] = jnp.broadcast_to(jnp.sum(diagonal, axis=0, keepdims=True), (8, 128))


def _unpacked(packed):
    row = lax.broadcasted_iota(jnp.int32, (64, 128), 0)
    lane = lax.broadcasted_iota(jnp.int32, (64, 128), 1)
    top = packed[0:64]
    diagonal = packed[64:65]
    turned = jnp.concatenate([top, top], axis=0).T
    upper_left = turned[0:64]
    bottom_left = turned[64:128]
    top_full = jnp.where(lane < row, upper_left, top)
    moved = pltpu.roll(top, 64, 1)
    bottom = jnp.where(lane > row + 64, upper_left, moved)
    bottom = jnp.where(lane == row + 64, diagonal, bottom)
    bottom = jnp.where(lane < 64, bottom_left, bottom)
    return jnp.concatenate([top_full, bottom], axis=0)


def _iterate_kernel(packed_ref, level_ref, weights_ref, *, total_rows):
    gram = _unpacked(packed_ref[...])
    scale = jnp.sqrt(jnp.sum(gram * gram, keepdims=True))
    level = gram / scale
    ident = (
        lax.broadcasted_iota(jnp.int32, (128, 128), 0) == lax.broadcasted_iota(jnp.int32, (128, 128), 1)
    ).astype(jnp.float32)

    def dot(a, b):
        return jnp.dot(a, b, precision=lax.Precision.HIGHEST, preferred_element_type=jnp.float32)

    inverse = ident
    for repeat in range(NS_ITERS):
        product = dot(inverse, level) if repeat else level
        factor = 1.5 * ident - 0.5 * product
        level = dot(level, factor)
        inverse = dot(factor, inverse) if repeat else factor
    level_ref[...] = level
    ratio = jnp.sqrt(jnp.float32(total_rows)) / jnp.sqrt(scale)
    weights_ref[...] = (inverse * ratio).astype(jnp.bfloat16)


def local(velocity, basis_old, strength, snapshots):
    modes = basis_old.shape[0]
    earlier_count = snapshots.shape[0]
    ranks = modes + earlier_count + 1
    head = (strength[:, None] * basis_old.reshape(modes, -1).astype(jnp.float32)).astype(jnp.bfloat16)
    field, newest = advance(velocity)
    newest = newest.reshape(1, -1).astype(jnp.bfloat16)
    whole = jnp.concatenate([head, snapshots.reshape(earlier_count, -1), newest], axis=0)
    gram = jnp.dot(whole, whole.T, preferred_element_type=jnp.float32)
    packed = pl.pallas_call(
        _pack_kernel,
        out_shape=jax.ShapeDtypeStruct((72, 128), jnp.float32),
        in_specs=[VMEM_SPEC],
        out_specs=VMEM_SPEC,
        name="pack",
    )(gram)
    packed = lax.psum(packed, ("grp", "gy", "gz"))
    total_rows = whole.shape[1] * lax.axis_size("grp") * lax.axis_size("gy") * lax.axis_size("gz")
    level, weights = pl.pallas_call(
        functools.partial(_iterate_kernel, total_rows=total_rows),
        out_shape=[
            jax.ShapeDtypeStruct((ranks, ranks), jnp.float32),
            jax.ShapeDtypeStruct((ranks, ranks), jnp.bfloat16),
        ],
        in_specs=[VMEM_SPEC],
        out_specs=[VMEM_SPEC] * 2,
        name="iterate",
    )(packed)
    basis_new = jnp.dot(weights, whole, preferred_element_type=jnp.float32).astype(jnp.bfloat16)
    basis_new = basis_new.reshape(ranks, 3, field.shape[1] // 2, field.shape[2] // 2, field.shape[3])
    return (field, basis_new, level)


def solution(mesh):
    placed = (
        P(None, "gy", "gz", "grp"),
        P(None, None, "gy", "gz", "grp"),
        P(),
        P(None, None, "gy", "gz", "grp"),
    )
    return jax.shard_map(
        local,
        mesh=mesh,
        in_specs=placed,
        out_specs=(P(None, "gy", "gz", "grp"), P(None, None, "gy", "gz", "grp"), P()),
        check_vma=False,
    )
```

time: 491 us -> 190 us (0.39)
  waiting for transfers between devices: 312 us -> 10.2 us
  blocking collectives: 0 us -> 113 us
  starting transfers between devices: 134 us -> 33.7 us
  Pallas kernels: 0 us -> 21.5 us
  between operations: 15.6 us -> 0.77 us
  other arithmetic: 11.5 us -> 0.9 us
  matrix products: 8.93 us -> 2.52 us
    psum x1 -> x0, waiting for transfers between devices: 276 us -> none  [local(): lax.psum(jnp.dot(whole, whole.T, preferred_element_type=jnp.float32), ('g...]
    psum x0 -> x1, blocking collectives: none -> 113 us  [local(): packed = lax.psum(packed, ('grp', 'gy', 'gz'))]
    ppermute x36 -> x6, starting transfers between devices: 134 us -> 33.7 us  [shift(): return lax.ppermute(x, axis, [(i, (i + step) % n) for i in range(n)])]
    ppermute x36 -> x6, waiting for transfers between devices: 35.6 us -> 10.2 us  [shift(): return lax.ppermute(x, axis, [(i, (i + step) % n) for i in range(n)])]
    pallas_call x0 -> x5, Pallas kernels: none -> 21.5 us  [the longest x1 10.9 us: advance(): pl.pallas_call(functools.partial(_stencil_kernel, last=lax.axis_size('gy'...]
    dot_general x25 -> x1, matrix products: 8.37 us -> 1.21 us  [local(): gram = jnp.dot(whole, whole.T, preferred_element_type=jnp.float32)]
    slice x12 -> x0, other arithmetic: 4.93 us -> none  [padded_2(): lax.slice_in_dim(block, block.shape[dim] - width, None, axis=dim)]
  transfers between devices with their start and end apart: 37 -> 6, of which waited for: 28 -> 3; matrix products, arithmetic and copies ran while one was open for 1% -> 1% of each run, Pallas kernels for 0% -> 0%
where the time goes in v1:
time: 190 us
  blocking collectives  113 us (59%)
  starting transfers between devices  33.7 us (18%)
  Pallas kernels  21.5 us (11%)
  waiting for transfers between devices  10.2 us (5%)
  local copies, waits for them, and re-layouts  6.75 us (4%)
  matrix products  2.52 us (1%)
    psum x1, blocking collectives, local(): packed = lax.psum(packed, ('grp', 'gy', 'gz'))  113 us
    ppermute x6, starting transfers between devices, shift(): return lax.ppermute(x, axis, [(i, (i + step) % n) for i in range(n)])  33.7 us
    pallas_call x1, Pallas kernels, advance(): pl.pallas_call(functools.partial(_stencil_kernel, last=lax.axis_size('gy'...  10.9 us
    ppermute x6, waiting for transfers between devices, shift(): return lax.ppermute(x, axis, [(i, (i + step) % n) for i in range(n)])  10.2 us
    pallas_call x1, Pallas kernels, local(): pl.pallas_call(functools.partial(_iterate_kernel, total_rows=total_rows),...  5 us
  transfers between devices with their start and end apart: 6, of which 3 were waited for; matrix products, arithmetic and copies ran while one was open for 1% of the time, Pallas kernels for 0%

profile of v1, /device:TPU:1, one launch (start us, length us, event | category | flops | bytes accessed | tf_op | source)
XLA Modules:
  0.0 189.7 jit_solution(5446841828297636734)
XLA Ops:
  0.6 8.0 %collective-permute-start.1 = (f32[3,8,8,128]{3,2,1,0:T(8,128)}, f32[3,8,8,128]{3,2,1,0:T(8,128)S(1)}, u32[]{:S(2)}, u32[]{:S(2)}) collective-permute-start(f32[3,8,8,128]{3,2,1,0:T(8,128)} %v_ref.5), channel_id=1, source_target_pairs={{0,15},{1,0},{2,1},{3,2},{4,3},{5,4},{6,5},{7,6},{8,7},{9,8},{10,9... | collective-permute-start | bytes 294920 | tf_op jit(solution)/shard_map/ppermute | solution.py:161
  8.7 1.9 %collective-permute-start = (f32[3,8,8,128]{3,2,1,0:T(8,128)}, f32[3,8,8,128]{3,2,1,0:T(8,128)S(1)}, u32[]{:S(2)}, u32[]{:S(2)}) collective-permute-start(f32[3,8,8,128]{3,2,1,0:T(8,128)} %v_ref.5), channel_id=1, source_target_pairs={{0,1},{1,2},{2,3},{3,4},{4,5},{5,6},{6,7},{7,8},{8,9},{9,10},{10,1... | collective-permute-start | bytes 294920 | tf_op jit(solution)/shard_map/ppermute | solution.py:161
  10.6 0.1 collective-permute-done.1.zh_ref
  10.7 0.0 copy-start.2
  10.7 5.6 %collective-permute-done.zl_ref = f32[3,8,8,128]{3,2,1,0:T(8,128)S(1)} collective-permute-done((f32[3,8,8,128]{3,2,1,0:T(8,128)}, f32[3,8,8,128]{3,2,1,0:T(8,128)S(1)}, u32[]{:S(2)}, u32[]{:S(2)}) %collective-permute-start) | collective-permute-done | bytes 98336 | tf_op jit(solution)/shard_map/ppermute | solution.py:161
  16.4 0.0 copy-done.2
  16.4 0.0 copy-start.3
  16.4 0.6 copy-done.3
  17.0 1.8 faces_y.1
  18.8 0.0 copy-start.7
  18.8 3.4 %collective-permute-start.2 = (f32[3,6,24,128]{3,2,1,0:T(8,128)}, f32[3,6,24,128]{3,2,1,0:T(8,128)S(1)}, u32[]{:S(2)}, u32[]{:S(2)}) collective-permute-start(f32[3,6,24,128]{3,2,1,0:T(8,128)} %get-tuple-element.11), channel_id=1, source_target_pairs={{0,16},{16,32},{32,48},{48,64},{64,80},{80,96},{96,112},{112,128},... | collective-permute-start | bytes 663560 | tf_op jit(solution)/shard_map/ppermute | solution.py:161
  22.2 5.8 %collective-permute-start.3 = (f32[3,6,24,128]{3,2,1,0:T(8,128)}, f32[3,6,24,128]{3,2,1,0:T(8,128)S(1)}, u32[]{:S(2)}, u32[]{:S(2)}) collective-permute-start(f32[3,6,24,128]{3,2,1,0:T(8,128)} %get-tuple-element.12), channel_id=1, source_target_pairs={{0,240},{16,0},{32,16},{48,32},{64,48},{80,64},{96,80},{112,96},{1... | collective-permute-start | bytes 663560 | tf_op jit(solution)/shard_map/ppermute | solution.py:161
  27.9 1.6 reshape.36
  29.6 0.0 copy-start.4
  29.6 0.0 collective-permute-done.2.yl_ref
  29.6 0.0 copy-start
  29.6 0.0 collective-permute-done.3.yh_ref
  29.6 0.7 copy-done
  30.3 0.0 copy-start.1
  30.3 0.7 copy-done.1
  31.0 2.2 %faces_x.1 = (f32[9,8,128]{2,1,0:T(8,128)}, f32[9,8,128]{2,1,0:T(8,128)}) custom-call(f32[3,8,8,128]{3,2,1,0:T(8,128)} %v_ref.5, f32[3,8,8,128]{3,2,1,0:T(8,128)} %copy-done.3, f32[3,8,8,128]{3,2,1,0:T(8,128)} %copy-done.2, f32[3,6,24,128]{3,2,1,0:T(8,128)} %copy-done, f32[3,6,24,128]{3,2,1,0:T(8,128)} %copy-done.1), custom_call_target="tpu_custom_call" | custom-call | tf_op jit(solution)/shard_map/faces_x/pallas_call | solution.py:177
  33.2 12.7 %collective-permute-start.4 = (f32[9,8,128]{2,1,0:T(8,128)}, f32[9,8,128]{2,1,0:T(8,128)S(1)}, u32[]{:S(2)}, u32[]{:S(2)}) collective-permute-start(f32[9,8,128]{2,1,0:T(8,128)} %get-tuple-element.13), channel_id=1, source_target_pairs={{0,768},{256,0},{512,256},{768,512},{1,769},{257,1},{513,257},{769... | collective-permute-start | bytes 110600 | tf_op jit(solution)/shard_map/ppermute | solution.py:161
  45.9 1.9 %collective-permute-start.5 = (f32[9,8,128]{2,1,0:T(8,128)}, f32[9,8,128]{2,1,0:T(8,128)S(1)}, u32[]{:S(2)}, u32[]{:S(2)}) collective-permute-start(f32[9,8,128]{2,1,0:T(8,128)} %get-tuple-element.14), channel_id=1, source_target_pairs={{0,256},{256,512},{512,768},{768,0},{1,257},{257,513},{513,769},{7... | collective-permute-start | bytes 110600 | tf_op jit(solution)/shard_map/ppermute | solution.py:161
  47.8 0.0 copy-done.7
  47.8 0.2 multiply_convert_fusion
  48.0 0.0 copy-done.4
  48.0 0.5 reshape.34
  48.5 0.0 collective-permute-done.4.xh_ref
  48.5 0.0 copy-start.5
  48.5 4.4 %collective-permute-done.5.xl_ref = f32[9,8,128]{2,1,0:T(8,128)S(1)} collective-permute-done((f32[9,8,128]{2,1,0:T(8,128)}, f32[9,8,128]{2,1,0:T(8,128)S(1)}, u32[]{:S(2)}, u32[]{:S(2)}) %collective-permute-start.5) | collective-permute-done | bytes 36896 | tf_op jit(solution)/shard_map/ppermute | solution.py:161
  52.9 0.0 copy-start.6
  52.9 0.0 copy-done.5
  52.9 0.6 copy-done.6
  53.5 10.9 %stencil.1 = (f32[3,8,8,128]{3,2,1,0:T(8,128)}, f32[3,4,4,128]{3,2,1,0:T(4,128)}) custom-call(s32[1]{0:T(128)} %bitcast.gy_ref, f32[3,8,8,128]{3,2,1,0:T(8,128)} %v_ref.5, f32[3,8,8,128]{3,2,1,0:T(8,128)} %copy-done.3, f32[3,8,8,128]{3,2,1,0:T(8,128)} %copy-done.2, f32[3,6,24,128]{3,2,1,0:T(8,128)} %copy-done, f32[3,6,24,128]{3,2,1,0:T(8,128)} %copy-done.1, ...), custom_call_target="tpu_custom_call" | custom-call | tf_op jit(solution)/shard_map/stencil/pallas_call | solution.py:187
  64.5 0.7 convert_element_type.29
  65.2 1.2 fusion.g_ref
  66.4 1.5 pack.1
  68.0 113.4 %psum.7.packed_ref = f32[72,128]{1,0:T(8,128)} all-reduce(f32[72,128]{1,0:T(8,128)} %pack.1), channel_id=1, replica_groups=mesh['grp'=4,'gy'=16,'gz'=16] {'grp','gy','gz'}, use_global_device_ids=true, to_apply=%region_0.0 | all-reduce | flops 9216 | bytes 73728 | tf_op jit(solution)/shard_map/psum | solution.py:261
  181.4 5.0 %iterate.1 = (f32[128,128]{1,0:T(8,128)}, bf16[128,128]{1,0:T(8,128)(2,1)}) custom-call(f32[72,128]{1,0:T(8,128)} %psum.7.packed_ref), custom_call_target="tpu_custom_call" | custom-call | tf_op jit(solution)/shard_map/iterate/pallas_call | solution.py:263
  186.4 1.3 convolution_convert_fusion
  187.7 2.0 %reshape.35 = bf16[128,3,4,4,128]{4,3,2,1,0:T(4,128)(2,1)} reshape(bf16[128,6144]{1,0:T(8,128)(2,1)S(1)} %convolution_convert_fusion) | data formatting | bytes 3145728 | tf_op jit(solution)/shard_map/reshape | solution.py:274
  (1 shorter events, 0.0 us)
Async XLA Ops:
  0.6 10.1 %collective-permute-start.1 = (f32[3,8,8,128]{3,2,1,0:T(8,128)}, f32[3,8,8,128]{3,2,1,0:T(8,128)S(1)}, u32[]{:S(2)}, u32[]{:S(2)}) collective-permute-start(f32[3,8,8,128]{3,2,1,0:T(8,128)} %v_ref.5), channel_id=1, source_target_pairs={{0,15},{1,0},{2,1},{3,2},{4,3},{5,4},{6,5},{7,6},{8,7},{9,8},{10,9... | collective-permute-start | bytes 294920 | tf_op jit(solution)/shard_map/ppermute | solution.py:161
  8.7 7.7 %collective-permute-start = (f32[3,8,8,128]{3,2,1,0:T(8,128)}, f32[3,8,8,128]{3,2,1,0:T(8,128)S(1)}, u32[]{:S(2)}, u32[]{:S(2)}) collective-permute-start(f32[3,8,8,128]{3,2,1,0:T(8,128)} %v_ref.5), channel_id=1, source_target_pairs={{0,1},{1,2},{2,3},{3,4},{4,5},{5,6},{6,7},{7,8},{8,9},{9,10},{10,1... | collective-permute-start | bytes 294920 | tf_op jit(solution)/shard_map/ppermute | solution.py:161
  10.7 5.6 %copy-start.2 = (f32[3,8,8,128]{3,2,1,0:T(8,128)}, f32[3,8,8,128]{3,2,1,0:T(8,128)S(1)}, u32[]{:S(2)}) copy-start(f32[3,8,8,128]{3,2,1,0:T(8,128)S(1)} %collective-permute-done.1.zh_ref) | copy-start | bytes 294916
  16.4 0.6 copy-start.3
  18.8 29.0 %copy-start.7 = (f32[64]{0:T(128)S(1)}, f32[64]{0:T(128)}, u32[]{:S(2)}) copy-start(f32[64]{0:T(128)} %param.6) | copy-start | bytes 772
  18.8 10.8 %collective-permute-start.2 = (f32[3,6,24,128]{3,2,1,0:T(8,128)}, f32[3,6,24,128]{3,2,1,0:T(8,128)S(1)}, u32[]{:S(2)}, u32[]{:S(2)}) collective-permute-start(f32[3,6,24,128]{3,2,1,0:T(8,128)} %get-tuple-element.11), channel_id=1, source_target_pairs={{0,16},{16,32},{32,48},{48,64},{64,80},{80,96},{96,112},{112,128},... | collective-permute-start | bytes 663560 | tf_op jit(solution)/shard_map/ppermute | solution.py:161
  22.2 7.4 %collective-permute-start.3 = (f32[3,6,24,128]{3,2,1,0:T(8,128)}, f32[3,6,24,128]{3,2,1,0:T(8,128)S(1)}, u32[]{:S(2)}, u32[]{:S(2)}) collective-permute-start(f32[3,6,24,128]{3,2,1,0:T(8,128)} %get-tuple-element.12), channel_id=1, source_target_pairs={{0,240},{16,0},{32,16},{48,32},{64,48},{80,64},{96,80},{112,96},{1... | collective-permute-start | bytes 663560 | tf_op jit(solution)/shard_map/ppermute | solution.py:161
  29.6 18.4 %copy-start.4 = (bf16[63,3,4,4,128]{4,3,2,1,0:T(4,128)(2,1)S(1)}, bf16[63,3,4,4,128]{4,3,2,1,0:T(4,128)(2,1)}, u32[]{:S(2)}) copy-start(bf16[63,3,4,4,128]{4,3,2,1,0:T(4,128)(2,1)} %param.7) | copy-start | bytes 2322436
  29.6 0.7 copy-start
  30.3 0.7 copy-start.1
  33.2 15.3 %collective-permute-start.4 = (f32[9,8,128]{2,1,0:T(8,128)}, f32[9,8,128]{2,1,0:T(8,128)S(1)}, u32[]{:S(2)}, u32[]{:S(2)}) collective-permute-start(f32[9,8,128]{2,1,0:T(8,128)} %get-tuple-element.13), channel_id=1, source_target_pairs={{0,768},{256,0},{512,256},{768,512},{1,769},{257,1},{513,257},{769... | collective-permute-start | bytes 110600 | tf_op jit(solution)/shard_map/ppermute | solution.py:161
  45.9 7.0 %collective-permute-start.5 = (f32[9,8,128]{2,1,0:T(8,128)}, f32[9,8,128]{2,1,0:T(8,128)S(1)}, u32[]{:S(2)}, u32[]{:S(2)}) collective-permute-start(f32[9,8,128]{2,1,0:T(8,128)} %get-tuple-element.14), channel_id=1, source_target_pairs={{0,256},{256,512},{512,768},{768,0},{1,257},{257,513},{513,769},{7... | collective-permute-start | bytes 110600 | tf_op jit(solution)/shard_map/ppermute | solution.py:161
  48.5 4.4 %copy-start.5 = (f32[9,8,128]{2,1,0:T(8,128)}, f32[9,8,128]{2,1,0:T(8,128)S(1)}, u32[]{:S(2)}) copy-start(f32[9,8,128]{2,1,0:T(8,128)S(1)} %collective-permute-done.4.xh_ref) | copy-start | bytes 110596
  52.9 0.6 copy-start.6

commit v2 on v1

--- a/solution.py
+++ b/solution.py
@@ -194,34 +194,22 @@
     )(gy, v, zl, zh, yl, yh, xh, xl)
 
 
-def _pack_kernel(g_ref, out_ref):
-    row = lax.broadcasted_iota(jnp.int32, (64, 128), 0)
-    lane = lax.broadcasted_iota(jnp.int32, (64, 128), 1)
-    top = g_ref[0:64, :]
-    bottom = g_ref[64:128, :]
-    out_ref[0:64, :] = jnp.where(lane < row, pltpu.roll(bottom, 64, 1), top)
-    diagonal = jnp.where(lane == row + 64, bottom, 0.0)
-    out_ref[64:72, :] = jnp.broadcast_to(jnp.sum(diagonal, axis=0, keepdims=True), (8, 128))
-
-
-def _unpacked(packed):
-    row = lax.broadcasted_iota(jnp.int32, (64, 128), 0)
-    lane = lax.broadcasted_iota(jnp.int32, (64, 128), 1)
-    top = packed[0:64]
-    diagonal = packed[64:65]
-    turned = jnp.concatenate([top, top], axis=0).T
-    upper_left = turned[0:64]
-    bottom_left = turned[64:128]
-    top_full = jnp.where(lane < row, upper_left, top)
-    moved = pltpu.roll(top, 64, 1)
-    bottom = jnp.where(lane > row + 64, upper_left, moved)
-    bottom = jnp.where(lane == row + 64, diagonal, bottom)
-    bottom = jnp.where(lane < 64, bottom_left, bottom)
-    return jnp.concatenate([top_full, bottom], axis=0)
-
-
-def _iterate_kernel(packed_ref, level_ref, weights_ref, *, total_rows):
-    gram = _unpacked(packed_ref[...])
+def exchanged(blocks, axes):
+    return lax.all_to_all(blocks, axes, 0, 0)
+
+
+def summed(gram):
+    lanes = gram.shape[1]
+    parts = lax.axis_size("gz")
+    rows = gram.shape[0] // parts
+    others = lax.axis_size("grp") * lax.axis_size("gy")
+    mine = jnp.sum(exchanged(gram.reshape(parts, rows, lanes), "gz"), axis=0)
+    mine = jnp.sum(exchanged(jnp.broadcast_to(mine[None], (others, rows, lanes)), ("grp", "gy")), axis=0)
+    return exchanged(jnp.broadcast_to(mine[None], (parts, rows, lanes)), "gz").reshape(gram.shape)
+
+
+def _iterate_kernel(gram_ref, level_ref, weights_ref, *, total_rows):
+    gram = gram_ref[...]
     scale = jnp.sqrt(jnp.sum(gram * gram, keepdims=True))
     level = gram / scale
     ident = (
@@ -251,14 +239,7 @@
     newest = newest.reshape(1, -1).astype(jnp.bfloat16)
     whole = jnp.concatenate([head, snapshots.reshape(earlier_count, -1), newest], axis=0)
     gram = jnp.dot(whole, whole.T, preferred_element_type=jnp.float32)
-    packed = pl.pallas_call(
-        _pack_kernel,
-        out_shape=jax.ShapeDtypeStruct((72, 128), jnp.float32),
-        in_specs=[VMEM_SPEC],
-        out_specs=VMEM_SPEC,
-        name="pack",
-    )(gram)
-    packed = lax.psum(packed, ("grp", "gy", "gz"))
+    gram = summed(gram)
     total_rows = whole.shape[1] * lax.axis_size("grp") * lax.axis_size("gy") * lax.axis_size("gz")
     level, weights = pl.pallas_call(
         functools.partial(_iterate_kernel, total_rows=total_rows),
@@ -269,7 +250,7 @@
         in_specs=[VMEM_SPEC],
         out_specs=[VMEM_SPEC] * 2,
         name="iterate",
-    )(packed)
+    )(gram)
     basis_new = jnp.dot(weights, whole, preferred_element_type=jnp.float32).astype(jnp.bfloat16)
     basis_new = basis_new.reshape(ranks, 3, field.shape[1] // 2, field.shape[2] // 2, field.shape[3])
     return (field, basis_new, level)

time: 190 us -> 121 us (0.64)
  blocking collectives: 113 us -> 46.5 us
    psum x1 -> x0, blocking collectives: 113 us -> none  [local(): packed = lax.psum(packed, ('grp', 'gy', 'gz'))]
    all_to_all x0 -> x3, blocking collectives: none -> 46.5 us  [exchanged(): return lax.all_to_all(blocks, axes, 0, 0)]
  transfers between devices with their start and end apart: 6 -> 6, of which waited for: 3 -> 3; matrix products, arithmetic and copies ran while one was open for 1% -> 2% of each run, Pallas kernels for 0% -> 0%
where the time goes in v2:
time: 121 us
  blocking collectives  46.5 us (38%)
  starting transfers between devices  33.7 us (28%)
  Pallas kernels  19.9 us (16%)
  waiting for transfers between devices  10.2 us (8%)
  local copies, waits for them, and re-layouts  6.8 us (6%)
  matrix products  1.88 us (2%)
    all_to_all x3, blocking collectives, exchanged(): return lax.all_to_all(blocks, axes, 0, 0)  46.5 us
    ppermute x6, starting transfers between devices, shift(): return lax.ppermute(x, axis, [(i, (i + step) % n) for i in range(n)])  33.7 us
    pallas_call x1, Pallas kernels, advance(): pl.pallas_call(functools.partial(_stencil_kernel, last=lax.axis_size('gy'...  10.9 us
    ppermute x6, waiting for transfers between devices, shift(): return lax.ppermute(x, axis, [(i, (i + step) % n) for i in range(n)])  10.2 us
    pallas_call x1, Pallas kernels, local(): pl.pallas_call(functools.partial(_iterate_kernel, total_rows=total_rows),...  4.97 us
    unnamed x16, local copies, waits for them, and re-layouts  2.63 us
  transfers between devices with their start and end apart: 6, of which 3 were waited for; matrix products, arithmetic and copies ran while one was open for 2% of the time, Pallas kernels for 0%

profile of v2, /device:TPU:1, one launch (start us, length us, event | category | flops | bytes accessed | tf_op | source)
XLA Modules:
  0.0 120.8 jit_solution(6201478461560945363)
XLA Ops:
  0.6 8.0 %collective-permute-start.1 = (f32[3,8,8,128]{3,2,1,0:T(8,128)}, f32[3,8,8,128]{3,2,1,0:T(8,128)S(1)}, u32[]{:S(2)}, u32[]{:S(2)}) collective-permute-start(f32[3,8,8,128]{3,2,1,0:T(8,128)} %v_ref.5), channel_id=1, source_target_pairs={{0,15},{1,0},{2,1},{3,2},{4,3},{5,4},{6,5},{7,6},{8,7},{9,8},{10,9... | collective-permute-start | bytes 294920 | tf_op jit(solution)/shard_map/ppermute | solution.py:161
  8.7 1.9 %collective-permute-start = (f32[3,8,8,128]{3,2,1,0:T(8,128)}, f32[3,8,8,128]{3,2,1,0:T(8,128)S(1)}, u32[]{:S(2)}, u32[]{:S(2)}) collective-permute-start(f32[3,8,8,128]{3,2,1,0:T(8,128)} %v_ref.5), channel_id=1, source_target_pairs={{0,1},{1,2},{2,3},{3,4},{4,5},{5,6},{6,7},{7,8},{8,9},{9,10},{10,1... | collective-permute-start | bytes 294920 | tf_op jit(solution)/shard_map/ppermute | solution.py:161
  10.6 0.1 collective-permute-done.1.zh_ref
  10.7 0.0 copy-start.2
  10.7 5.6 %collective-permute-done.zl_ref = f32[3,8,8,128]{3,2,1,0:T(8,128)S(1)} collective-permute-done((f32[3,8,8,128]{3,2,1,0:T(8,128)}, f32[3,8,8,128]{3,2,1,0:T(8,128)S(1)}, u32[]{:S(2)}, u32[]{:S(2)}) %collective-permute-start) | collective-permute-done | bytes 98336 | tf_op jit(solution)/shard_map/ppermute | solution.py:161
  16.4 0.0 copy-done.2
  16.4 0.0 copy-start.3
  16.4 0.6 copy-done.3
  17.0 1.8 %faces_y.1 = (f32[3,6,24,128]{3,2,1,0:T(8,128)}, f32[3,6,24,128]{3,2,1,0:T(8,128)}) custom-call(f32[3,8,8,128]{3,2,1,0:T(8,128)} %v_ref.5, f32[3,8,8,128]{3,2,1,0:T(8,128)} %copy-done.3, f32[3,8,8,128]{3,2,1,0:T(8,128)} %copy-done.2), custom_call_target="tpu_custom_call" | custom-call | tf_op jit(solution)/shard_map/faces_y/pallas_call | solution.py:168
  18.8 0.0 copy-start.7
  18.8 3.4 %collective-permute-start.2 = (f32[3,6,24,128]{3,2,1,0:T(8,128)}, f32[3,6,24,128]{3,2,1,0:T(8,128)S(1)}, u32[]{:S(2)}, u32[]{:S(2)}) collective-permute-start(f32[3,6,24,128]{3,2,1,0:T(8,128)} %get-tuple-element.11), channel_id=1, source_target_pairs={{0,16},{16,32},{32,48},{48,64},{64,80},{80,96},{96,112},{112,128},... | collective-permute-start | bytes 663560 | tf_op jit(solution)/shard_map/ppermute | solution.py:161
  22.2 5.8 %collective-permute-start.3 = (f32[3,6,24,128]{3,2,1,0:T(8,128)}, f32[3,6,24,128]{3,2,1,0:T(8,128)S(1)}, u32[]{:S(2)}, u32[]{:S(2)}) collective-permute-start(f32[3,6,24,128]{3,2,1,0:T(8,128)} %get-tuple-element.12), channel_id=1, source_target_pairs={{0,240},{16,0},{32,16},{48,32},{64,48},{80,64},{96,80},{112,96},{1... | collective-permute-start | bytes 663560 | tf_op jit(solution)/shard_map/ppermute | solution.py:161
  27.9 1.6 %reshape.46 = f32[64,6144]{1,0:T(8,128)S(1)} reshape(bf16[64,3,4,4,128]{4,3,2,1,0:T(4,128)(2,1)} %param.5) | data formatting | bytes 2359296 | tf_op jit(solution)/shard_map/convert_element_type | solution.py:237
  29.6 0.0 copy-start.4
  29.6 0.0 collective-permute-done.2.yl_ref
  29.6 0.0 copy-start
  29.6 0.0 collective-permute-done.3.yh_ref
  29.6 0.7 copy-done
  30.3 0.0 copy-start.1
  30.3 0.7 copy-done.1
  31.0 2.2 %faces_x.1 = (f32[9,8,128]{2,1,0:T(8,128)}, f32[9,8,128]{2,1,0:T(8,128)}) custom-call(f32[3,8,8,128]{3,2,1,0:T(8,128)} %v_ref.5, f32[3,8,8,128]{3,2,1,0:T(8,128)} %copy-done.3, f32[3,8,8,128]{3,2,1,0:T(8,128)} %copy-done.2, f32[3,6,24,128]{3,2,1,0:T(8,128)} %copy-done, f32[3,6,24,128]{3,2,1,0:T(8,128)} %copy-done.1), custom_call_target="tpu_custom_call" | custom-call | tf_op jit(solution)/shard_map/faces_x/pallas_call | solution.py:177
  33.3 12.6 %collective-permute-start.4 = (f32[9,8,128]{2,1,0:T(8,128)}, f32[9,8,128]{2,1,0:T(8,128)S(1)}, u32[]{:S(2)}, u32[]{:S(2)}) collective-permute-start(f32[9,8,128]{2,1,0:T(8,128)} %get-tuple-element.13), channel_id=1, source_target_pairs={{0,768},{256,0},{512,256},{768,512},{1,769},{257,1},{513,257},{769... | collective-permute-start | bytes 110600 | tf_op jit(solution)/shard_map/ppermute | solution.py:161
  45.9 1.9 %collective-permute-start.5 = (f32[9,8,128]{2,1,0:T(8,128)}, f32[9,8,128]{2,1,0:T(8,128)S(1)}, u32[]{:S(2)}, u32[]{:S(2)}) collective-permute-start(f32[9,8,128]{2,1,0:T(8,128)} %get-tuple-element.14), channel_id=1, source_target_pairs={{0,256},{256,512},{512,768},{768,0},{1,257},{257,513},{513,769},{7... | collective-permute-start | bytes 110600 | tf_op jit(solution)/shard_map/ppermute | solution.py:161
  47.8 0.0 copy-done.7
  47.8 0.2 multiply_convert_fusion
  48.0 0.0 copy-done.4
  48.0 0.5 reshape.42
  48.5 0.0 collective-permute-done.4.xh_ref
  48.5 0.0 copy-start.5
  48.5 4.4 %collective-permute-done.5.xl_ref = f32[9,8,128]{2,1,0:T(8,128)S(1)} collective-permute-done((f32[9,8,128]{2,1,0:T(8,128)}, f32[9,8,128]{2,1,0:T(8,128)S(1)}, u32[]{:S(2)}, u32[]{:S(2)}) %collective-permute-start.5) | collective-permute-done | bytes 36896 | tf_op jit(solution)/shard_map/ppermute | solution.py:161
  52.9 0.0 copy-start.6
  52.9 0.0 copy-done.5
  52.9 0.6 copy-done.6
  53.5 10.9 %stencil.1 = (f32[3,8,8,128]{3,2,1,0:T(8,128)}, f32[3,4,4,128]{3,2,1,0:T(4,128)}) custom-call(s32[1]{0:T(128)} %bitcast.gy_ref, f32[3,8,8,128]{3,2,1,0:T(8,128)} %v_ref.5, f32[3,8,8,128]{3,2,1,0:T(8,128)} %copy-done.3, f32[3,8,8,128]{3,2,1,0:T(8,128)} %copy-done.2, f32[3,6,24,128]{3,2,1,0:T(8,128)} %copy-done, f32[3,6,24,128]{3,2,1,0:T(8,128)} %copy-done.1, ...), custom_call_target="tpu_custom_call" | custom-call | tf_op jit(solution)/shard_map/stencil/pallas_call | solution.py:187
  64.5 0.7 convert_element_type.29
  65.2 0.6 convolution_bitcast_fusion
  65.8 10.5 %all_to_all.15 = f32[16,8,128]{2,1,0:T(8,128)S(1)} all-to-all(f32[16,8,128]{2,1,0:T(8,128)S(1)} %convolution_bitcast_fusion), channel_id=1, replica_groups=mesh['grp'=4,'gy'=16,'gz'=16] {'gz'}, dimensions={0} | all-to-all | bytes 131072 | tf_op jit(solution)/shard_map/all_to_all | solution.py:198
  76.4 25.4 %all_to_all.16 = f32[64,8,128]{2,1,0:T(8,128)S(1)} all-to-all(f32[64,8,128]{2,1,0:T(8,128)S(1)} %broadcast_in_dim.4), channel_id=1, replica_groups=mesh['grp'=4,'gy'=16,'gz'=16] {'grp','gy'}, dimensions={0} | all-to-all | bytes 524288 | tf_op jit(solution)/shard_map/all_to_all | solution.py:198
  101.7 0.1 reduce_sum.19
  101.8 10.6 %all_to_all.17 = f32[16,8,128]{2,1,0:T(8,128)} all-to-all(f32[16,8,128]{2,1,0:T(8,128)S(1)} %broadcast_in_dim.5), channel_id=1, replica_groups=mesh['grp'=4,'gy'=16,'gz'=16] {'gz'}, dimensions={0} | all-to-all | bytes 131072 | tf_op jit(solution)/shard_map/all_to_all | solution.py:198
  112.5 5.0 %iterate.1 = (f32[128,128]{1,0:T(8,128)}, bf16[128,128]{1,0:T(8,128)(2,1)}) custom-call(f32[128,128]{1,0:T(8,128)} %bitcast.5), custom_call_target="tpu_custom_call" | custom-call | tf_op jit(solution)/shard_map/iterate/pallas_call | solution.py:244
  117.4 1.3 %convolution_convert_fusion = bf16[128,6144]{1,0:T(8,128)(2,1)S(1)} fusion(bf16[128,128]{1,0:T(8,128)(2,1)} %get-tuple-element.17, bf16[1,6144]{1,0:T(2,128)(2,1)S(1)} %convert_element_type.30, bf16[63,6144]{1,0:T(8,128)(2,1)S(1)} %reshape.42, bf16[64,6144]{1,0:T(8,128)(2,1)S(1)} %multiply_convert_fusion), kind=kOutput, calls=%fused_computation | convolution fusion | flops 206831616 | bytes 3178496 | tf_op jit(solution)/shard_map/dot_general | solution.py:254
  118.7 2.0 %reshape.45 = bf16[128,3,4,4,128]{4,3,2,1,0:T(4,128)(2,1)} reshape(bf16[128,6144]{1,0:T(8,128)(2,1)S(1)} %convolution_convert_fusion) | data formatting | bytes 3145728 | tf_op jit(solution)/shard_map/reshape | solution.py:255
  (4 shorter events, 0.1 us)
Async XLA Ops:
  0.6 10.1 %collective-permute-start.1 = (f32[3,8,8,128]{3,2,1,0:T(8,128)}, f32[3,8,8,128]{3,2,1,0:T(8,128)S(1)}, u32[]{:S(2)}, u32[]{:S(2)}) collective-permute-start(f32[3,8,8,128]{3,2,1,0:T(8,128)} %v_ref.5), channel_id=1, source_target_pairs={{0,15},{1,0},{2,1},{3,2},{4,3},{5,4},{6,5},{7,6},{8,7},{9,8},{10,9... | collective-permute-start | bytes 294920 | tf_op jit(solution)/shard_map/ppermute | solution.py:161
  8.7 7.7 %collective-permute-start = (f32[3,8,8,128]{3,2,1,0:T(8,128)}, f32[3,8,8,128]{3,2,1,0:T(8,128)S(1)}, u32[]{:S(2)}, u32[]{:S(2)}) collective-permute-start(f32[3,8,8,128]{3,2,1,0:T(8,128)} %v_ref.5), channel_id=1, source_target_pairs={{0,1},{1,2},{2,3},{3,4},{4,5},{5,6},{6,7},{7,8},{8,9},{9,10},{10,1... | collective-permute-start | bytes 294920 | tf_op jit(solution)/shard_map/ppermute | solution.py:161
  10.7 5.6 %copy-start.2 = (f32[3,8,8,128]{3,2,1,0:T(8,128)}, f32[3,8,8,128]{3,2,1,0:T(8,128)S(1)}, u32[]{:S(2)}) copy-start(f32[3,8,8,128]{3,2,1,0:T(8,128)S(1)} %collective-permute-done.1.zh_ref) | copy-start | bytes 294916
  16.4 0.6 copy-start.3
  18.8 29.0 %copy-start.7 = (f32[64]{0:T(128)S(1)}, f32[64]{0:T(128)}, u32[]{:S(2)}) copy-start(f32[64]{0:T(128)} %param.6) | copy-start | bytes 772
  18.8 10.8 %collective-permute-start.2 = (f32[3,6,24,128]{3,2,1,0:T(8,128)}, f32[3,6,24,128]{3,2,1,0:T(8,128)S(1)}, u32[]{:S(2)}, u32[]{:S(2)}) collective-permute-start(f32[3,6,24,128]{3,2,1,0:T(8,128)} %get-tuple-element.11), channel_id=1, source_target_pairs={{0,16},{16,32},{32,48},{48,64},{64,80},{80,96},{96,112},{112,128},... | collective-permute-start | bytes 663560 | tf_op jit(solution)/shard_map/ppermute | solution.py:161
  22.2 7.4 %collective-permute-start.3 = (f32[3,6,24,128]{3,2,1,0:T(8,128)}, f32[3,6,24,128]{3,2,1,0:T(8,128)S(1)}, u32[]{:S(2)}, u32[]{:S(2)}) collective-permute-start(f32[3,6,24,128]{3,2,1,0:T(8,128)} %get-tuple-element.12), channel_id=1, source_target_pairs={{0,240},{16,0},{32,16},{48,32},{64,48},{80,64},{96,80},{112,96},{1... | collective-permute-start | bytes 663560 | tf_op jit(solution)/shard_map/ppermute | solution.py:161
  29.6 18.4 %copy-start.4 = (bf16[63,3,4,4,128]{4,3,2,1,0:T(4,128)(2,1)S(1)}, bf16[63,3,4,4,128]{4,3,2,1,0:T(4,128)(2,1)}, u32[]{:S(2)}) copy-start(bf16[63,3,4,4,128]{4,3,2,1,0:T(4,128)(2,1)} %param.7) | copy-start | bytes 2322436
  29.6 0.7 copy-start
  30.3 0.7 copy-start.1
  33.3 15.2 %collective-permute-start.4 = (f32[9,8,128]{2,1,0:T(8,128)}, f32[9,8,128]{2,1,0:T(8,128)S(1)}, u32[]{:S(2)}, u32[]{:S(2)}) collective-permute-start(f32[9,8,128]{2,1,0:T(8,128)} %get-tuple-element.13), channel_id=1, source_target_pairs={{0,768},{256,0},{512,256},{768,512},{1,769},{257,1},{513,257},{769... | collective-permute-start | bytes 110600 | tf_op jit(solution)/shard_map/ppermute | solution.py:161
  45.9 7.0 %collective-permute-start.5 = (f32[9,8,128]{2,1,0:T(8,128)}, f32[9,8,128]{2,1,0:T(8,128)S(1)}, u32[]{:S(2)}, u32[]{:S(2)}) collective-permute-start(f32[9,8,128]{2,1,0:T(8,128)} %get-tuple-element.14), channel_id=1, source_target_pairs={{0,256},{256,512},{512,768},{768,0},{1,257},{257,513},{513,769},{7... | collective-permute-start | bytes 110600 | tf_op jit(solution)/shard_map/ppermute | solution.py:161
  48.5 4.4 %copy-start.5 = (f32[9,8,128]{2,1,0:T(8,128)}, f32[9,8,128]{2,1,0:T(8,128)S(1)}, u32[]{:S(2)}) copy-start(f32[9,8,128]{2,1,0:T(8,128)S(1)} %collective-permute-done.4.xh_ref) | copy-start | bytes 110596
  52.9 0.6 copy-start.6

commit v3 on v2

--- a/solution.py
+++ b/solution.py
@@ -118,7 +118,7 @@
             ref[:, HALO + 8] = jnp.zeros((3, 2, 40, 128), jnp.float32)
 
     def stage(source, target, combine, depth):
-        @pl.loop(depth, PLANES - depth)
+        @pl.loop(depth, PLANES - depth, unroll=2)
         def _(y):
             for row in (8, 16, 24):
                 moved = _euler(source, y, row, 2)
@@ -152,6 +152,10 @@
             new_ref[c, y // 2] = adv_ref[c, y, pl.ds(0, 4, stride=2), :]
 
 
+def near(x):
+    return pltpu.with_memory_space_constraint(x, pltpu.VMEM)
+
+
 VMEM_SPEC = pl.BlockSpec(memory_space=pltpu.VMEM)
 SMEM_SPEC = pl.BlockSpec(memory_space=pltpu.SMEM)
 
@@ -167,45 +171,49 @@
     zh = shift(v, "gz", -1)
     low, high = pl.pallas_call(
         _faces_y_kernel,
-        out_shape=[jax.ShapeDtypeStruct((3, HALO, 24, 128), f32)] * 2,
+        out_shape=[pltpu.VMEM((3, HALO, 24, 128), f32)] * 2,
         in_specs=[VMEM_SPEC] * 3,
         out_specs=[VMEM_SPEC] * 2,
         name="faces_y",
-    )(v, zl, zh)
+    )(*map(near, (v, zl, zh)))
     yl = shift(high, "gy", 1)
     yh = shift(low, "gy", -1)
     low, high = pl.pallas_call(
         _faces_x_kernel,
-        out_shape=[jax.ShapeDtypeStruct((9, 8, 128), f32)] * 2,
+        out_shape=[pltpu.VMEM((9, 8, 128), f32)] * 2,
         in_specs=[VMEM_SPEC] * 5,
         out_specs=[VMEM_SPEC] * 2,
         name="faces_x",
-    )(v, zl, zh, yl, yh)
+    )(*map(near, (v, zl, zh, yl, yh)))
     xl = shift(high, "grp", 1)
     xh = shift(low, "grp", -1)
     gy = lax.axis_index("gy").astype(jnp.int32).reshape(1)
     return pl.pallas_call(
         functools.partial(_stencil_kernel, last=lax.axis_size("gy") - 1),
-        out_shape=[jax.ShapeDtypeStruct((3, 8, 8, 128), f32), jax.ShapeDtypeStruct((3, 4, 4, 128), f32)],
+        out_shape=[jax.ShapeDtypeStruct((3, 8, 8, 128), f32), pltpu.VMEM((3, 4, 4, 128), f32)],
         in_specs=[SMEM_SPEC] + [VMEM_SPEC] * 7,
         out_specs=[VMEM_SPEC] * 2,
         scratch_shapes=[pltpu.VMEM((3, PLANES, 2, 40, 128), f32)] * 3,
         name="stencil",
-    )(gy, v, zl, zh, yl, yh, xh, xl)
-
-
-def exchanged(blocks, axes):
-    return lax.all_to_all(blocks, axes, 0, 0)
+    )(gy, *map(near, (v, zl, zh, yl, yh, xh, xl)))
+
+
+def exchanged(blocks, axes, groups):
+    return lax.all_to_all(blocks, axes, 0, 0, axis_index_groups=groups)
 
 
 def summed(gram):
     lanes = gram.shape[1]
-    parts = lax.axis_size("gz")
+    slow, mid, fast = (lax.axis_size(a) for a in ("grp", "gy", "gz"))
+    parts, others = 2 * fast, slow * mid // 2
     rows = gram.shape[0] // parts
-    others = lax.axis_size("grp") * lax.axis_size("gy")
-    mine = jnp.sum(exchanged(gram.reshape(parts, rows, lanes), "gz"), axis=0)
-    mine = jnp.sum(exchanged(jnp.broadcast_to(mine[None], (others, rows, lanes)), ("grp", "gy")), axis=0)
-    return exchanged(jnp.broadcast_to(mine[None], (parts, rows, lanes)), "gz").reshape(gram.shape)
+    near_groups = [[parts * i + j for j in range(parts)] for i in range(mid // 2)]
+    far_groups = [[2 * i + core for i in range(others)] for core in range(2)]
+    mine = jnp.sum(exchanged(gram.reshape(parts, rows, lanes), ("gy", "gz"), near_groups), axis=0)
+    spread = jnp.broadcast_to(mine[None], (others, rows, lanes))
+    mine = jnp.sum(exchanged(spread, ("grp", "gy"), far_groups), axis=0)
+    spread = jnp.broadcast_to(mine[None], (parts, rows, lanes))
+    return exchanged(spread, ("gy", "gz"), near_groups).reshape(gram.shape)
 
 
 def _iterate_kernel(gram_ref, level_ref, weights_ref, *, total_rows):
@@ -245,12 +253,12 @@
         functools.partial(_iterate_kernel, total_rows=total_rows),
         out_shape=[
             jax.ShapeDtypeStruct((ranks, ranks), jnp.float32),
-            jax.ShapeDtypeStruct((ranks, ranks), jnp.bfloat16),
+            pltpu.VMEM((ranks, ranks), jnp.bfloat16),
         ],
         in_specs=[VMEM_SPEC],
         out_specs=[VMEM_SPEC] * 2,
         name="iterate",
-    )(gram)
+    )(near(gram))
     basis_new = jnp.dot(weights, whole, preferred_element_type=jnp.float32).astype(jnp.bfloat16)
     basis_new = basis_new.reshape(ranks, 3, field.shape[1] // 2, field.shape[2] // 2, field.shape[3])
     return (field, basis_new, level)

time: 121 us -> 109 us (0.901)
  Pallas kernels: 19.9 us -> 11.6 us
  waiting for transfers between devices: 10.2 us -> 7.77 us
    pallas_call x1, Pallas kernels: 10.9 us -> 7.06 us  [advance(): pl.pallas_call(functools.partial(_stencil_kernel, last=lax.axis_size('gy'...]
    pallas_call x2, Pallas kernels: 4.04 us -> 0.46 us  [the longest x1 0.43 us: advance(): pl.pallas_call(_faces_x_kernel, out_shape=[pltpu.VMEM((9, 8, 128), f32)]...]
    ppermute x6, waiting for transfers between devices: 10.2 us -> 7.77 us  [shift(): return lax.ppermute(x, axis, [(i, (i + step) % n) for i in range(n)])]
    unnamed x16 -> x6, local copies, waits for them, and re-layouts: 2.63 us -> 0.9 us
    reshape x1, local copies, waits for them, and re-layouts: 0.45 us -> 1.81 us  [local(): snapshots.reshape(earlier_count, -1)]
  transfers between devices with their start and end apart: 6 -> 6, of which waited for: 3 -> 3; matrix products, arithmetic and copies ran while one was open for 2% -> 4% of each run, Pallas kernels for 0% -> 0%
where the time goes in v3:
time: 109 us; the launch traced here: 108 us
  blocking collectives  45.4 us (42%)
  starting transfers between devices  34.2 us (31%)
  Pallas kernels  11.6 us (11%)
  waiting for transfers between devices  7.77 us (7%)
  local copies, waits for them, and re-layouts  6.42 us (6%)
  other arithmetic  1.13 us (1%)
  matrix products  1.13 us (1%)
    all_to_all x3, blocking collectives, exchanged(): return lax.all_to_all(blocks, axes, 0, 0, axis_index_groups=groups)  45.4 us
    ppermute x6, starting transfers between devices, shift(): return lax.ppermute(x, axis, [(i, (i + step) % n) for i in range(n)])  34.2 us
    ppermute x6, waiting for transfers between devices, shift(): return lax.ppermute(x, axis, [(i, (i + step) % n) for i in range(n)])  7.77 us
    pallas_call x1, Pallas kernels, advance(): pl.pallas_call(functools.partial(_stencil_kernel, last=lax.axis_size('gy'...  7.06 us
    pallas_call x1, Pallas kernels, local(): pl.pallas_call(functools.partial(_iterate_kernel, total_rows=total_rows),...  4.12 us
  transfers between devices with their start and end apart: 6, of which 3 were waited for; matrix products, arithmetic and copies ran while one was open for 4% of the time, Pallas kernels for 0%

profile of v3, /device:TPU:1, one launch (start us, length us, event | category | flops | bytes accessed | tf_op | source)
XLA Modules:
  0.0 108.4 jit_solution(11248480368293922220)
XLA Ops:
  0.6 8.0 %collective-permute-start.1 = (f32[3,8,8,128]{3,2,1,0:T(8,128)}, f32[3,8,8,128]{3,2,1,0:T(8,128)S(1)}, u32[]{:S(2)}, u32[]{:S(2)}) collective-permute-start(f32[3,8,8,128]{3,2,1,0:T(8,128)} %v_ref.5), channel_id=1, source_target_pairs={{0,15},{1,0},{2,1},{3,2},{4,3},{5,4},{6,5},{7,6},{8,7},{9,8},{10,9... | collective-permute-start | bytes 294920 | tf_op jit(solution)/shard_map/ppermute | solution.py:165
  8.7 1.9 %collective-permute-start = (f32[3,8,8,128]{3,2,1,0:T(8,128)}, f32[3,8,8,128]{3,2,1,0:T(8,128)S(1)}, u32[]{:S(2)}, u32[]{:S(2)}) collective-permute-start(f32[3,8,8,128]{3,2,1,0:T(8,128)} %v_ref.5), channel_id=1, source_target_pairs={{0,1},{1,2},{2,3},{3,4},{4,5},{5,6},{6,7},{7,8},{8,9},{9,10},{10,1... | collective-permute-start | bytes 294920 | tf_op jit(solution)/shard_map/ppermute | solution.py:165
  10.6 0.1 collective-permute-done.1.zh_ref
  10.7 5.6 %collective-permute-done.zl_ref = f32[3,8,8,128]{3,2,1,0:T(8,128)S(1)} collective-permute-done((f32[3,8,8,128]{3,2,1,0:T(8,128)}, f32[3,8,8,128]{3,2,1,0:T(8,128)S(1)}, u32[]{:S(2)}, u32[]{:S(2)}) %collective-permute-start) | collective-permute-done | bytes 98336 | tf_op jit(solution)/shard_map/ppermute | solution.py:165
  16.4 0.0 copy-start
  16.4 0.9 copy-done
  17.3 0.0 copy-start.2
  17.3 3.4 %collective-permute-start.2 = (f32[3,6,24,128]{3,2,1,0:T(8,128)S(1)}, f32[3,6,24,128]{3,2,1,0:T(8,128)S(1)}, u32[]{:S(2)}, u32[]{:S(2)}) collective-permute-start(f32[3,6,24,128]{3,2,1,0:T(8,128)S(1)} %get-tuple-element.11), channel_id=1, source_target_pairs={{0,16},{16,32},{32,48},{48,64},{64,80},{80,96},{96,112},{112,128},... | collective-permute-start | bytes 663560 | tf_op jit(solution)/shard_map/ppermute | solution.py:165
  20.7 5.8 %collective-permute-start.3 = (f32[3,6,24,128]{3,2,1,0:T(8,128)S(1)}, f32[3,6,24,128]{3,2,1,0:T(8,128)S(1)}, u32[]{:S(2)}, u32[]{:S(2)}) collective-permute-start(f32[3,6,24,128]{3,2,1,0:T(8,128)S(1)} %get-tuple-element.12), channel_id=1, source_target_pairs={{0,240},{16,0},{32,16},{48,32},{64,48},{80,64},{96,80},{112,96},{1... | collective-permute-start | bytes 663560 | tf_op jit(solution)/shard_map/ppermute | solution.py:165
  26.5 1.6 %reshape.46 = f32[64,6144]{1,0:T(8,128)S(1)} reshape(bf16[64,3,4,4,128]{4,3,2,1,0:T(4,128)(2,1)} %param.5) | data formatting | bytes 2359296 | tf_op jit(solution)/shard_map/convert_element_type | solution.py:245
  28.1 0.0 collective-permute-done.2.yl_ref
  28.1 0.0 collective-permute-done.3.yh_ref
  28.2 0.4 faces_x.1
  28.6 13.1 %collective-permute-start.4 = (f32[9,8,128]{2,1,0:T(8,128)S(1)}, f32[9,8,128]{2,1,0:T(8,128)S(1)}, u32[]{:S(2)}, u32[]{:S(2)}) collective-permute-start(f32[9,8,128]{2,1,0:T(8,128)S(1)} %get-tuple-element.13), channel_id=1, source_target_pairs={{0,768},{256,0},{512,256},{768,512},{1,769},{257,1},{513,257},{769... | collective-permute-start | bytes 110600 | tf_op jit(solution)/shard_map/ppermute | solution.py:165
  41.7 1.9 %collective-permute-start.5 = (f32[9,8,128]{2,1,0:T(8,128)S(1)}, f32[9,8,128]{2,1,0:T(8,128)S(1)}, u32[]{:S(2)}, u32[]{:S(2)}) collective-permute-start(f32[9,8,128]{2,1,0:T(8,128)S(1)} %get-tuple-element.14), channel_id=1, source_target_pairs={{0,256},{256,512},{512,768},{768,0},{1,257},{257,513},{513,769},{7... | collective-permute-start | bytes 110600 | tf_op jit(solution)/shard_map/ppermute | solution.py:165
  43.7 0.0 copy-done.2
  43.7 1.0 multiply_convert_fusion
  44.7 0.0 copy-start.1
  44.7 1.8 %reshape.42 = bf16[63,6144]{1,0:T(8,128)(2,1)S(1)} reshape(bf16[63,3,4,4,128]{4,3,2,1,0:T(4,128)(2,1)} %param.7) | data formatting | bytes 1548288 | tf_op jit(solution)/shard_map/reshape | solution.py:248
  46.5 0.0 collective-permute-done.4.xh_ref
  46.5 2.0 %collective-permute-done.5.xl_ref = f32[9,8,128]{2,1,0:T(8,128)S(1)} collective-permute-done((f32[9,8,128]{2,1,0:T(8,128)S(1)}, f32[9,8,128]{2,1,0:T(8,128)S(1)}, u32[]{:S(2)}, u32[]{:S(2)}) %collective-permute-start.5) | collective-permute-done | bytes 36896 | tf_op jit(solution)/shard_map/ppermute | solution.py:165
  48.5 7.1 %stencil.1 = (f32[3,8,8,128]{3,2,1,0:T(8,128)}, f32[3,4,4,128]{3,2,1,0:T(4,128)S(1)}) custom-call(s32[1]{0:T(128)} %bitcast.gy_ref, f32[3,8,8,128]{3,2,1,0:T(8,128)S(1)} %copy-done, f32[3,8,8,128]{3,2,1,0:T(8,128)S(1)} %collective-permute-done.zl_ref, f32[3,8,8,128]{3,2,1,0:T(8,128)S(1)} %collective-permute-done.1.zh_ref, ...), custom_call_target="tpu_custom_call" | custom-call | tf_op jit(solution)/shard_map/stencil/pallas_call | solution.py:191
  55.6 0.0 copy-done.1
  55.6 0.6 fusion
  56.2 13.1 %all_to_all.15 = f32[32,4,128]{2,1,0:T(4,128)S(1)} all-to-all(f32[32,4,128]{2,1,0:T(4,128)S(1)} %bitcast.5), channel_id=1, replica_groups={{0,1,2,3,4,5,6,7,8,9,10,11,12,13,14,15,16,17,18,19,20,21,22,23,24,25,26..., dimensions={0} | all-to-all | bytes 131072 | tf_op jit(solution)/shard_map/all_to_all | solution.py:202
  69.3 19.1 %all_to_all.16 = f32[32,4,128]{2,1,0:T(4,128)S(1)} all-to-all(f32[32,4,128]{2,1,0:T(4,128)S(1)} %broadcast_in_dim.4), channel_id=1, replica_groups={{0,32,64,96,128,160,192,224,256,288,320,352,384,416,448,480,512,544,576..., dimensions={0} | all-to-all | bytes 131072 | tf_op jit(solution)/shard_map/all_to_all | solution.py:202
  88.5 13.2 %all_to_all.17 = f32[32,4,128]{2,1,0:T(4,128)S(1)} all-to-all(f32[32,4,128]{2,1,0:T(4,128)S(1)} %broadcast_in_dim.5), channel_id=1, replica_groups={{0,1,2,3,4,5,6,7,8,9,10,11,12,13,14,15,16,17,18,19,20,21,22,23,24,25,26..., dimensions={0} | all-to-all | bytes 131072 | tf_op jit(solution)/shard_map/all_to_all | solution.py:202
  101.7 4.1 %iterate.1 = (f32[128,128]{1,0:T(8,128)}, bf16[128,128]{1,0:T(8,128)(2,1)S(1)}) custom-call(f32[128,128]{1,0:T(8,128)S(1)} %bitcast.4), custom_call_target="tpu_custom_call" | custom-call | tf_op jit(solution)/shard_map/iterate/pallas_call | solution.py:252
  105.8 0.6 convolution_convert_fusion
  106.4 2.0 %reshape.45 = bf16[128,3,4,4,128]{4,3,2,1,0:T(4,128)(2,1)} reshape(bf16[128,6144]{1,0:T(8,128)(2,1)S(1)} %convolution_convert_fusion) | data formatting | bytes 3145728 | tf_op jit(solution)/shard_map/reshape | solution.py:263
  (7 shorter events, 0.2 us)
Async XLA Ops:
  0.6 10.1 %collective-permute-start.1 = (f32[3,8,8,128]{3,2,1,0:T(8,128)}, f32[3,8,8,128]{3,2,1,0:T(8,128)S(1)}, u32[]{:S(2)}, u32[]{:S(2)}) collective-permute-start(f32[3,8,8,128]{3,2,1,0:T(8,128)} %v_ref.5), channel_id=1, source_target_pairs={{0,15},{1,0},{2,1},{3,2},{4,3},{5,4},{6,5},{7,6},{8,7},{9,8},{10,9... | collective-permute-start | bytes 294920 | tf_op jit(solution)/shard_map/ppermute | solution.py:165
  8.7 7.7 %collective-permute-start = (f32[3,8,8,128]{3,2,1,0:T(8,128)}, f32[3,8,8,128]{3,2,1,0:T(8,128)S(1)}, u32[]{:S(2)}, u32[]{:S(2)}) collective-permute-start(f32[3,8,8,128]{3,2,1,0:T(8,128)} %v_ref.5), channel_id=1, source_target_pairs={{0,1},{1,2},{2,3},{3,4},{4,5},{5,6},{6,7},{7,8},{8,9},{9,10},{10,1... | collective-permute-start | bytes 294920 | tf_op jit(solution)/shard_map/ppermute | solution.py:165
  16.4 0.9 copy-start
  17.3 26.4 %copy-start.2 = (f32[64]{0:T(128)S(1)}, f32[64]{0:T(128)}, u32[]{:S(2)}) copy-start(f32[64]{0:T(128)} %param.6) | copy-start | bytes 772
  17.3 10.8 %collective-permute-start.2 = (f32[3,6,24,128]{3,2,1,0:T(8,128)S(1)}, f32[3,6,24,128]{3,2,1,0:T(8,128)S(1)}, u32[]{:S(2)}, u32[]{:S(2)}) collective-permute-start(f32[3,6,24,128]{3,2,1,0:T(8,128)S(1)} %get-tuple-element.11), channel_id=1, source_target_pairs={{0,16},{16,32},{32,48},{48,64},{64,80},{80,96},{96,112},{112,128},... | collective-permute-start | bytes 663560 | tf_op jit(solution)/shard_map/ppermute | solution.py:165
  20.7 7.4 %collective-permute-start.3 = (f32[3,6,24,128]{3,2,1,0:T(8,128)S(1)}, f32[3,6,24,128]{3,2,1,0:T(8,128)S(1)}, u32[]{:S(2)}, u32[]{:S(2)}) collective-permute-start(f32[3,6,24,128]{3,2,1,0:T(8,128)S(1)} %get-tuple-element.12), channel_id=1, source_target_pairs={{0,240},{16,0},{32,16},{48,32},{64,48},{80,64},{96,80},{112,96},{1... | collective-permute-start | bytes 663560 | tf_op jit(solution)/shard_map/ppermute | solution.py:165
  28.6 17.9 %collective-permute-start.4 = (f32[9,8,128]{2,1,0:T(8,128)S(1)}, f32[9,8,128]{2,1,0:T(8,128)S(1)}, u32[]{:S(2)}, u32[]{:S(2)}) collective-permute-start(f32[9,8,128]{2,1,0:T(8,128)S(1)} %get-tuple-element.13), channel_id=1, source_target_pairs={{0,768},{256,0},{512,256},{768,512},{1,769},{257,1},{513,257},{769... | collective-permute-start | bytes 110600 | tf_op jit(solution)/shard_map/ppermute | solution.py:165
  41.7 6.8 %collective-permute-start.5 = (f32[9,8,128]{2,1,0:T(8,128)S(1)}, f32[9,8,128]{2,1,0:T(8,128)S(1)}, u32[]{:S(2)}, u32[]{:S(2)}) collective-permute-start(f32[9,8,128]{2,1,0:T(8,128)S(1)} %get-tuple-element.14), channel_id=1, source_target_pairs={{0,256},{256,512},{512,768},{768,0},{1,257},{257,513},{513,769},{7... | collective-permute-start | bytes 110600 | tf_op jit(solution)/shard_map/ppermute | solution.py:165
  44.7 10.9 %copy-start.1 = (bf16[64,6144]{1,0:T(8,128)(2,1)S(1)}, bf16[64,6144]{1,0:T(8,128)(2,1)}, u32[]{:S(2)}) copy-start(bf16[64,6144]{1,0:T(8,128)(2,1)} %multiply_convert_fusion) | copy-start | bytes 2359300

commit v4 on v3

--- a/solution.py
+++ b/solution.py
@@ -118,13 +118,22 @@
             ref[:, HALO + 8] = jnp.zeros((3, 2, 40, 128), jnp.float32)
 
     def stage(source, target, combine, depth):
-        @pl.loop(depth, PLANES - depth, unroll=2)
+        def plane(y, middle, outer):
+            for row, tiles in ((8, outer), (16, middle), (24, outer)):
+                if tiles:
+                    moved = _euler(source, y, row, tiles)
+                    for c in range(3):
+                        for t in range(tiles):
+                            target[c, y, t, row : row + 8, :] = combine(moved[c][t], c, y, t, row)
+
+        plane(depth, 1, 0)
+        plane(PLANES - 1 - depth, 1, 0)
+        plane(depth + 1, 2, 1)
+        plane(PLANES - 2 - depth, 2, 1)
+
+        @pl.loop(depth + 2, PLANES - 2 - depth, unroll=2)
         def _(y):
-            for row in (8, 16, 24):
-                moved = _euler(source, y, row, 2)
-                for c in range(3):
-                    for t in range(2):
-                        target[c, y, t, row : row + 8, :] = combine(moved[c][t], c, y, t, row)
+            plane(y, 2, 2)
 
         close(target)
 
@@ -169,6 +178,7 @@
     f32 = jnp.float32
     zl = shift(v, "gz", 1)
     zh = shift(v, "gz", -1)
+    v = jnp.where(lax.axis_index("gy") >= 0, v, 0.0)
     low, high = pl.pallas_call(
         _faces_y_kernel,
         out_shape=[pltpu.VMEM((3, HALO, 24, 128), f32)] * 2,

time: 109 us -> 107 us (0.982)
  local copies, waits for them, and re-layouts: 6.42 us -> 4.18 us
    reshape x1, local copies, waits for them, and re-layouts: 1.81 us -> 0.45 us  [local(): snapshots.reshape(earlier_count, -1)]
  transfers between devices with their start and end apart: 6 -> 6, of which waited for: 3 -> 2; matrix products, arithmetic and copies ran while one was open for 4% -> 4% of each run, Pallas kernels for 0% -> 0%
where the time goes in v4:
time: 107 us; the launch traced here: 106 us
  blocking collectives  45 us (42%)
  starting transfers between devices  34.2 us (32%)
  Pallas kernels  10.9 us (10%)
  waiting for transfers between devices  8.2 us (8%)
  local copies, waits for them, and re-layouts  4.18 us (4%)
  other arithmetic  2.04 us (2%)
  matrix products  1.13 us (1%)
    all_to_all x3, blocking collectives, exchanged(): return lax.all_to_all(blocks, axes, 0, 0, axis_index_groups=groups)  45 us
    ppermute x6, starting transfers between devices, shift(): return lax.ppermute(x, axis, [(i, (i + step) % n) for i in range(n)])  34.2 us
    ppermute x6, waiting for transfers between devices, shift(): return lax.ppermute(x, axis, [(i, (i + step) % n) for i in range(n)])  8.2 us
    pallas_call x1, Pallas kernels, advance(): pl.pallas_call(functools.partial(_stencil_kernel, last=lax.axis_size('gy'...  6.28 us
    pallas_call x1, Pallas kernels, local(): pl.pallas_call(functools.partial(_iterate_kernel, total_rows=total_rows),...  4.13 us
  transfers between devices with their start and end apart: 6, of which 2 were waited for; matrix products, arithmetic and copies ran while one was open for 4% of the time, Pallas kernels for 0%

profile of v4, /device:TPU:1, one launch (start us, length us, event | category | flops | bytes accessed | tf_op | source)
XLA Modules:
  0.0 106.3 jit_solution(14143573490852885408)
XLA Ops:
  0.6 8.0 %collective-permute-start.1 = (f32[3,8,8,128]{3,2,1,0:T(8,128)}, f32[3,8,8,128]{3,2,1,0:T(8,128)S(1)}, u32[]{:S(2)}, u32[]{:S(2)}) collective-permute-start(f32[3,8,8,128]{3,2,1,0:T(8,128)} %param.4), channel_id=1, source_target_pairs={{0,15},{1,0},{2,1},{3,2},{4,3},{5,4},{6,5},{7,6},{8,7},{9,8},{10,9... | collective-permute-start | bytes 294920 | tf_op jit(solution)/shard_map/ppermute | solution.py:174
  8.7 1.9 %collective-permute-start = (f32[3,8,8,128]{3,2,1,0:T(8,128)}, f32[3,8,8,128]{3,2,1,0:T(8,128)S(1)}, u32[]{:S(2)}, u32[]{:S(2)}) collective-permute-start(f32[3,8,8,128]{3,2,1,0:T(8,128)} %param.4), channel_id=1, source_target_pairs={{0,1},{1,2},{2,3},{3,4},{4,5},{5,6},{6,7},{7,8},{8,9},{9,10},{10,1... | collective-permute-start | bytes 294920 | tf_op jit(solution)/shard_map/ppermute | solution.py:174
  10.6 0.9 broadcast_select_fusion.v_ref
  11.5 0.0 collective-permute-done.1.zh_ref
  11.5 4.8 %collective-permute-done.zl_ref = f32[3,8,8,128]{3,2,1,0:T(8,128)S(1)} collective-permute-done((f32[3,8,8,128]{3,2,1,0:T(8,128)}, f32[3,8,8,128]{3,2,1,0:T(8,128)S(1)}, u32[]{:S(2)}, u32[]{:S(2)}) %collective-permute-start) | collective-permute-done | bytes 98336 | tf_op jit(solution)/shard_map/ppermute | solution.py:174
  16.4 0.0 copy-start.2
  16.4 3.4 %collective-permute-start.2 = (f32[3,6,24,128]{3,2,1,0:T(8,128)S(1)}, f32[3,6,24,128]{3,2,1,0:T(8,128)S(1)}, u32[]{:S(2)}, u32[]{:S(2)}) collective-permute-start(f32[3,6,24,128]{3,2,1,0:T(8,128)S(1)} %get-tuple-element.11), channel_id=1, source_target_pairs={{0,16},{16,32},{32,48},{48,64},{64,80},{80,96},{96,112},{112,128},... | collective-permute-start | bytes 663560 | tf_op jit(solution)/shard_map/ppermute | solution.py:174
  19.8 5.8 %collective-permute-start.3 = (f32[3,6,24,128]{3,2,1,0:T(8,128)S(1)}, f32[3,6,24,128]{3,2,1,0:T(8,128)S(1)}, u32[]{:S(2)}, u32[]{:S(2)}) collective-permute-start(f32[3,6,24,128]{3,2,1,0:T(8,128)S(1)} %get-tuple-element.12), channel_id=1, source_target_pairs={{0,240},{16,0},{32,16},{48,32},{64,48},{80,64},{96,80},{112,96},{1... | collective-permute-start | bytes 663560 | tf_op jit(solution)/shard_map/ppermute | solution.py:174
  25.6 1.6 %reshape.46 = f32[64,6144]{1,0:T(8,128)S(1)} reshape(bf16[64,3,4,4,128]{4,3,2,1,0:T(4,128)(2,1)} %param.5) | data formatting | bytes 2359296 | tf_op jit(solution)/shard_map/convert_element_type | solution.py:255
  27.2 0.0 copy-start.1
  27.3 0.0 collective-permute-done.2.yl_ref
  27.3 0.0 collective-permute-done.3.yh_ref
  27.3 0.4 faces_x.1
  27.7 13.1 %collective-permute-start.4 = (f32[9,8,128]{2,1,0:T(8,128)S(1)}, f32[9,8,128]{2,1,0:T(8,128)S(1)}, u32[]{:S(2)}, u32[]{:S(2)}) collective-permute-start(f32[9,8,128]{2,1,0:T(8,128)S(1)} %get-tuple-element.13), channel_id=1, source_target_pairs={{0,768},{256,0},{512,256},{768,512},{1,769},{257,1},{513,257},{769... | collective-permute-start | bytes 110600 | tf_op jit(solution)/shard_map/ppermute | solution.py:174
  40.8 1.9 %collective-permute-start.5 = (f32[9,8,128]{2,1,0:T(8,128)S(1)}, f32[9,8,128]{2,1,0:T(8,128)S(1)}, u32[]{:S(2)}, u32[]{:S(2)}) collective-permute-start(f32[9,8,128]{2,1,0:T(8,128)S(1)} %get-tuple-element.14), channel_id=1, source_target_pairs={{0,256},{256,512},{512,768},{768,0},{1,257},{257,513},{513,769},{7... | collective-permute-start | bytes 110600 | tf_op jit(solution)/shard_map/ppermute | solution.py:174
  42.8 0.0 copy-done.2
  42.8 1.0 multiply_convert_fusion
  43.8 0.0 copy-done.1
  43.8 0.0 copy-start
  43.8 0.5 reshape.42
  44.3 0.0 collective-permute-done.4.xh_ref
  44.3 3.4 %collective-permute-done.5.xl_ref = f32[9,8,128]{2,1,0:T(8,128)S(1)} collective-permute-done((f32[9,8,128]{2,1,0:T(8,128)S(1)}, f32[9,8,128]{2,1,0:T(8,128)S(1)}, u32[]{:S(2)}, u32[]{:S(2)}) %collective-permute-start.5) | collective-permute-done | bytes 36896 | tf_op jit(solution)/shard_map/ppermute | solution.py:174
  47.6 6.3 %stencil.1 = (f32[3,8,8,128]{3,2,1,0:T(8,128)}, f32[3,4,4,128]{3,2,1,0:T(4,128)S(1)}) custom-call(s32[1]{0:T(128)} %bitcast.gy_ref, f32[3,8,8,128]{3,2,1,0:T(8,128)S(1)} %broadcast_select_fusion.v_ref, f32[3,8,8,128]{3,2,1,0:T(8,128)S(1)} %collective-permute-done.zl_ref, f32[3,8,8,128]{3,2,1,0:T(8,128)S(1)} %collective-permute-done.1.zh_ref, ...), custom_call_target="tpu_custom_call" | custom-call | tf_op jit(solution)/shard_map/stencil/pallas_call | solution.py:201
  53.9 0.0 copy-done
  53.9 0.6 fusion
  54.5 13.1 %all_to_all.15 = f32[32,4,128]{2,1,0:T(4,128)S(1)} all-to-all(f32[32,4,128]{2,1,0:T(4,128)S(1)} %bitcast.5), channel_id=1, replica_groups={{0,1,2,3,4,5,6,7,8,9,10,11,12,13,14,15,16,17,18,19,20,21,22,23,24,25,26..., dimensions={0} | all-to-all | bytes 131072 | tf_op jit(solution)/shard_map/all_to_all | solution.py:212
  67.7 18.7 %all_to_all.16 = f32[32,4,128]{2,1,0:T(4,128)S(1)} all-to-all(f32[32,4,128]{2,1,0:T(4,128)S(1)} %broadcast_in_dim.9), channel_id=1, replica_groups={{0,32,64,96,128,160,192,224,256,288,320,352,384,416,448,480,512,544,576..., dimensions={0} | all-to-all | bytes 131072 | tf_op jit(solution)/shard_map/all_to_all | solution.py:212
  86.4 13.2 %all_to_all.17 = f32[32,4,128]{2,1,0:T(4,128)S(1)} all-to-all(f32[32,4,128]{2,1,0:T(4,128)S(1)} %broadcast_in_dim.10), channel_id=1, replica_groups={{0,1,2,3,4,5,6,7,8,9,10,11,12,13,14,15,16,17,18,19,20,21,22,23,24,25,26..., dimensions={0} | all-to-all | bytes 131072 | tf_op jit(solution)/shard_map/all_to_all | solution.py:212
  99.6 4.1 %iterate.1 = (f32[128,128]{1,0:T(8,128)}, bf16[128,128]{1,0:T(8,128)(2,1)S(1)}) custom-call(f32[128,128]{1,0:T(8,128)S(1)} %bitcast.4), custom_call_target="tpu_custom_call" | custom-call | tf_op jit(solution)/shard_map/iterate/pallas_call | solution.py:262
  103.7 0.6 convolution_convert_fusion
  104.3 2.0 %reshape.45 = bf16[128,3,4,4,128]{4,3,2,1,0:T(4,128)(2,1)} reshape(bf16[128,6144]{1,0:T(8,128)(2,1)S(1)} %convolution_convert_fusion) | data formatting | bytes 3145728 | tf_op jit(solution)/shard_map/reshape | solution.py:273
  (7 shorter events, 0.2 us)
Async XLA Ops:
  0.6 10.9 %collective-permute-start.1 = (f32[3,8,8,128]{3,2,1,0:T(8,128)}, f32[3,8,8,128]{3,2,1,0:T(8,128)S(1)}, u32[]{:S(2)}, u32[]{:S(2)}) collective-permute-start(f32[3,8,8,128]{3,2,1,0:T(8,128)} %param.4), channel_id=1, source_target_pairs={{0,15},{1,0},{2,1},{3,2},{4,3},{5,4},{6,5},{7,6},{8,7},{9,8},{10,9... | collective-permute-start | bytes 294920 | tf_op jit(solution)/shard_map/ppermute | solution.py:174
  8.7 7.7 %collective-permute-start = (f32[3,8,8,128]{3,2,1,0:T(8,128)}, f32[3,8,8,128]{3,2,1,0:T(8,128)S(1)}, u32[]{:S(2)}, u32[]{:S(2)}) collective-permute-start(f32[3,8,8,128]{3,2,1,0:T(8,128)} %param.4), channel_id=1, source_target_pairs={{0,1},{1,2},{2,3},{3,4},{4,5},{5,6},{6,7},{7,8},{8,9},{9,10},{10,1... | collective-permute-start | bytes 294920 | tf_op jit(solution)/shard_map/ppermute | solution.py:174
  16.4 26.4 %copy-start.2 = (f32[64]{0:T(128)S(1)}, f32[64]{0:T(128)}, u32[]{:S(2)}) copy-start(f32[64]{0:T(128)} %param.6) | copy-start | bytes 772
  16.4 10.9 %collective-permute-start.2 = (f32[3,6,24,128]{3,2,1,0:T(8,128)S(1)}, f32[3,6,24,128]{3,2,1,0:T(8,128)S(1)}, u32[]{:S(2)}, u32[]{:S(2)}) collective-permute-start(f32[3,6,24,128]{3,2,1,0:T(8,128)S(1)} %get-tuple-element.11), channel_id=1, source_target_pairs={{0,16},{16,32},{32,48},{48,64},{64,80},{80,96},{96,112},{112,128},... | collective-permute-start | bytes 663560 | tf_op jit(solution)/shard_map/ppermute | solution.py:174
  19.8 7.5 %collective-permute-start.3 = (f32[3,6,24,128]{3,2,1,0:T(8,128)S(1)}, f32[3,6,24,128]{3,2,1,0:T(8,128)S(1)}, u32[]{:S(2)}, u32[]{:S(2)}) collective-permute-start(f32[3,6,24,128]{3,2,1,0:T(8,128)S(1)} %get-tuple-element.12), channel_id=1, source_target_pairs={{0,240},{16,0},{32,16},{48,32},{64,48},{80,64},{96,80},{112,96},{1... | collective-permute-start | bytes 663560 | tf_op jit(solution)/shard_map/ppermute | solution.py:174
  27.2 16.6 %copy-start.1 = (bf16[63,3,4,4,128]{4,3,2,1,0:T(4,128)(2,1)S(1)}, bf16[63,3,4,4,128]{4,3,2,1,0:T(4,128)(2,1)}, u32[]{:S(2)}) copy-start(bf16[63,3,4,4,128]{4,3,2,1,0:T(4,128)(2,1)} %param.7) | copy-start | bytes 2322436
  27.7 16.6 %collective-permute-start.4 = (f32[9,8,128]{2,1,0:T(8,128)S(1)}, f32[9,8,128]{2,1,0:T(8,128)S(1)}, u32[]{:S(2)}, u32[]{:S(2)}) collective-permute-start(f32[9,8,128]{2,1,0:T(8,128)S(1)} %get-tuple-element.13), channel_id=1, source_target_pairs={{0,768},{256,0},{512,256},{768,512},{1,769},{257,1},{513,257},{769... | collective-permute-start | bytes 110600 | tf_op jit(solution)/shard_map/ppermute | solution.py:174
  40.8 6.8 %collective-permute-start.5 = (f32[9,8,128]{2,1,0:T(8,128)S(1)}, f32[9,8,128]{2,1,0:T(8,128)S(1)}, u32[]{:S(2)}, u32[]{:S(2)}) collective-permute-start(f32[9,8,128]{2,1,0:T(8,128)S(1)} %get-tuple-element.14), channel_id=1, source_target_pairs={{0,256},{256,512},{512,768},{768,0},{1,257},{257,513},{513,769},{7... | collective-permute-start | bytes 110600 | tf_op jit(solution)/shard_map/ppermute | solution.py:174
  43.8 10.1 %copy-start = (bf16[64,6144]{1,0:T(8,128)(2,1)S(1)}, bf16[64,6144]{1,0:T(8,128)(2,1)}, u32[]{:S(2)}) copy-start(bf16[64,6144]{1,0:T(8,128)(2,1)} %multiply_convert_fusion) | copy-start | bytes 2359300

commit v5 on v4

--- a/solution.py
+++ b/solution.py
@@ -62,10 +62,13 @@
     return plus, minus
 
 
-def _euler(u_ref, y, row, tiles):
+def _euler(u_ref, y, row, tiles, share):
     lane = _lanes()
+    spread = share * DT * VISC
     u = [[u_ref[c, y, t, row : row + 8, :] for t in range(2)] for c in range(3)]
-    half = [[u[c][t] * (0.5 * DT) for t in range(tiles)] for c in range(3)]
+    half = [[u[c][t] * (share * 0.5 * DT) for t in range(tiles)] for c in range(3)]
+    ahead = [[spread - half[c][t] for t in range(tiles)] for c in range(3)]
+    behind = [[spread + half[c][t] for t in range(tiles)] for c in range(3)]
     out = []
     for c in range(3):
         plus, minus = _rotated(u[c], lane)
@@ -75,13 +78,10 @@
             ym = u_ref[c, y - 1, t, row : row + 8, :]
             zp = u_ref[c, y, t, row + 1 : row + 9, :]
             zm = u_ref[c, y, t, row - 1 : row + 7, :]
-            carried = (
-                half[0][t] * (plus[t] - minus[t])
-                + half[1][t] * (yp - ym)
-                + half[2][t] * (zp - zm)
+            outs.append(
+                (u[c][t] * (share - 6.0 * spread) + (plus[t] * ahead[0][t] + minus[t] * behind[0][t]))
+                + ((yp * ahead[1][t] + ym * behind[1][t]) + (zp * ahead[2][t] + zm * behind[2][t]))
             )
-            around = (plus[t] + minus[t]) + (yp + ym) + (zp + zm)
-            outs.append(u[c][t] + ((DT * VISC) * (around - 6.0 * u[c][t]) - carried))
         out.append(outs)
     return out
 
@@ -117,14 +117,17 @@
         def _():
             ref[:, HALO + 8] = jnp.zeros((3, 2, 40, 128), jnp.float32)
 
-    def stage(source, target, combine, depth):
+    def stage(source, target, own, share, depth):
         def plane(y, middle, outer):
             for row, tiles in ((8, outer), (16, middle), (24, outer)):
                 if tiles:
-                    moved = _euler(source, y, row, tiles)
+                    moved = _euler(source, y, row, tiles, share)
                     for c in range(3):
                         for t in range(tiles):
-                            target[c, y, t, row : row + 8, :] = combine(moved[c][t], c, y, t, row)
+                            value = moved[c][t]
+                            if own:
+                                value = value + own * a_ref[c, y, t, row : row + 8, :]
+                            target[c, y, t, row : row + 8, :] = value
 
         plane(depth, 1, 0)
         plane(PLANES - 1 - depth, 1, 0)
@@ -137,25 +140,16 @@
 
         close(target)
 
-    def keep(w, c, y, t, row):
-        return w
-
-    def quarter(w, c, y, t, row):
-        return 0.75 * a_ref[c, y, t, row : row + 8, :] + 0.25 * w
-
-    def third(w, c, y, t, row):
-        return a_ref[c, y, t, row : row + 8, :] * (1.0 / 3.0) + (2.0 / 3.0) * w
-
     close(a_ref)
-    stage(a_ref, b_ref, keep, 1)
-    stage(b_ref, c_ref, quarter, 2)
-    stage(c_ref, a_ref, third, 3)
-    stage(a_ref, b_ref, keep, 4)
-    stage(b_ref, c_ref, quarter, 5)
+    stage(a_ref, b_ref, 0.0, 1.0, 1)
+    stage(b_ref, c_ref, 0.75, 0.25, 2)
+    stage(c_ref, a_ref, 1.0 / 3.0, 2.0 / 3.0, 3)
+    stage(a_ref, b_ref, 0.0, 1.0, 4)
+    stage(b_ref, c_ref, 0.75, 0.25, 5)
     for y in range(HALO, HALO + 8):
-        moved = _euler(c_ref, y, 16, 1)
+        moved = _euler(c_ref, y, 16, 1, 2.0 / 3.0)
         for c in range(3):
-            adv_ref[c, y - HALO] = third(moved[c][0], c, y, 0, 16)
+            adv_ref[c, y - HALO] = moved[c][0] + a_ref[c, y, 0, 16:24, :] * (1.0 / 3.0)
     for c in range(3):
         for y in range(0, 8, 2):
             new_ref[c, y // 2] = adv_ref[c, y, pl.ds(0, 4, stride=2), :]

time: 107 us -> 106 us (level)
  no operation moved by 1% of the time
where the time goes in v5:
time: 106 us
  blocking collectives  45 us (42%)
  starting transfers between devices  34.2 us (32%)
  Pallas kernels  10.5 us (10%)
  waiting for transfers between devices  8.2 us (8%)
  local copies, waits for them, and re-layouts  4.18 us (4%)
  other arithmetic  2.04 us (2%)
  matrix products  1.13 us (1%)
    all_to_all x3, blocking collectives, exchanged(): return lax.all_to_all(blocks, axes, 0, 0, axis_index_groups=groups)  45 us
    ppermute x6, starting transfers between devices, shift(): return lax.ppermute(x, axis, [(i, (i + step) % n) for i in range(n)])  34.2 us
    ppermute x6, waiting for transfers between devices, shift(): return lax.ppermute(x, axis, [(i, (i + step) % n) for i in range(n)])  8.2 us
    pallas_call x1, Pallas kernels, advance(): pl.pallas_call(functools.partial(_stencil_kernel, last=lax.axis_size('gy'...  5.88 us
    pallas_call x1, Pallas kernels, local(): pl.pallas_call(functools.partial(_iterate_kernel, total_rows=total_rows),...  4.13 us
  transfers between devices with their start and end apart: 6, of which 2 were waited for; matrix products, arithmetic and copies ran while one was open for 4% of the time, Pallas kernels for 0%

profile of v5, /device:TPU:1, one launch (start us, length us, event | category | flops | bytes accessed | tf_op | source)
XLA Modules:
  0.0 105.9 jit_solution(16887394985688551470)
XLA Ops:
  0.6 8.0 %collective-permute-start.1 = (f32[3,8,8,128]{3,2,1,0:T(8,128)}, f32[3,8,8,128]{3,2,1,0:T(8,128)S(1)}, u32[]{:S(2)}, u32[]{:S(2)}) collective-permute-start(f32[3,8,8,128]{3,2,1,0:T(8,128)} %param.4), channel_id=1, source_target_pairs={{0,15},{1,0},{2,1},{3,2},{4,3},{5,4},{6,5},{7,6},{8,7},{9,8},{10,9... | collective-permute-start | bytes 294920 | tf_op jit(solution)/shard_map/ppermute | solution.py:168
  8.7 1.9 %collective-permute-start = (f32[3,8,8,128]{3,2,1,0:T(8,128)}, f32[3,8,8,128]{3,2,1,0:T(8,128)S(1)}, u32[]{:S(2)}, u32[]{:S(2)}) collective-permute-start(f32[3,8,8,128]{3,2,1,0:T(8,128)} %param.4), channel_id=1, source_target_pairs={{0,1},{1,2},{2,3},{3,4},{4,5},{5,6},{6,7},{7,8},{8,9},{9,10},{10,1... | collective-permute-start | bytes 294920 | tf_op jit(solution)/shard_map/ppermute | solution.py:168
  10.6 0.9 broadcast_select_fusion.v_ref
  11.5 0.0 collective-permute-done.1.zh_ref
  11.5 4.8 %collective-permute-done.zl_ref = f32[3,8,8,128]{3,2,1,0:T(8,128)S(1)} collective-permute-done((f32[3,8,8,128]{3,2,1,0:T(8,128)}, f32[3,8,8,128]{3,2,1,0:T(8,128)S(1)}, u32[]{:S(2)}, u32[]{:S(2)}) %collective-permute-start) | collective-permute-done | bytes 98336 | tf_op jit(solution)/shard_map/ppermute | solution.py:168
  16.4 0.0 copy-start.2
  16.4 3.4 %collective-permute-start.2 = (f32[3,6,24,128]{3,2,1,0:T(8,128)S(1)}, f32[3,6,24,128]{3,2,1,0:T(8,128)S(1)}, u32[]{:S(2)}, u32[]{:S(2)}) collective-permute-start(f32[3,6,24,128]{3,2,1,0:T(8,128)S(1)} %get-tuple-element.11), channel_id=1, source_target_pairs={{0,16},{16,32},{32,48},{48,64},{64,80},{80,96},{96,112},{112,128},... | collective-permute-start | bytes 663560 | tf_op jit(solution)/shard_map/ppermute | solution.py:168
  19.8 5.8 %collective-permute-start.3 = (f32[3,6,24,128]{3,2,1,0:T(8,128)S(1)}, f32[3,6,24,128]{3,2,1,0:T(8,128)S(1)}, u32[]{:S(2)}, u32[]{:S(2)}) collective-permute-start(f32[3,6,24,128]{3,2,1,0:T(8,128)S(1)} %get-tuple-element.12), channel_id=1, source_target_pairs={{0,240},{16,0},{32,16},{48,32},{64,48},{80,64},{96,80},{112,96},{1... | collective-permute-start | bytes 663560 | tf_op jit(solution)/shard_map/ppermute | solution.py:168
  25.6 1.6 %reshape.46 = f32[64,6144]{1,0:T(8,128)S(1)} reshape(bf16[64,3,4,4,128]{4,3,2,1,0:T(4,128)(2,1)} %param.5) | data formatting | bytes 2359296 | tf_op jit(solution)/shard_map/convert_element_type | solution.py:249
  27.2 0.0 copy-start.1
  27.3 0.0 collective-permute-done.2.yl_ref
  27.3 0.0 collective-permute-done.3.yh_ref
  27.3 0.4 faces_x.1
  27.7 13.1 %collective-permute-start.4 = (f32[9,8,128]{2,1,0:T(8,128)S(1)}, f32[9,8,128]{2,1,0:T(8,128)S(1)}, u32[]{:S(2)}, u32[]{:S(2)}) collective-permute-start(f32[9,8,128]{2,1,0:T(8,128)S(1)} %get-tuple-element.13), channel_id=1, source_target_pairs={{0,768},{256,0},{512,256},{768,512},{1,769},{257,1},{513,257},{769... | collective-permute-start | bytes 110600 | tf_op jit(solution)/shard_map/ppermute | solution.py:168
  40.8 1.9 %collective-permute-start.5 = (f32[9,8,128]{2,1,0:T(8,128)S(1)}, f32[9,8,128]{2,1,0:T(8,128)S(1)}, u32[]{:S(2)}, u32[]{:S(2)}) collective-permute-start(f32[9,8,128]{2,1,0:T(8,128)S(1)} %get-tuple-element.14), channel_id=1, source_target_pairs={{0,256},{256,512},{512,768},{768,0},{1,257},{257,513},{513,769},{7... | collective-permute-start | bytes 110600 | tf_op jit(solution)/shard_map/ppermute | solution.py:168
  42.8 0.0 copy-done.2
  42.8 1.0 multiply_convert_fusion
  43.8 0.0 copy-done.1
  43.8 0.0 copy-start
  43.8 0.5 reshape.42
  44.3 0.0 collective-permute-done.4.xh_ref
  44.3 3.4 %collective-permute-done.5.xl_ref = f32[9,8,128]{2,1,0:T(8,128)S(1)} collective-permute-done((f32[9,8,128]{2,1,0:T(8,128)S(1)}, f32[9,8,128]{2,1,0:T(8,128)S(1)}, u32[]{:S(2)}, u32[]{:S(2)}) %collective-permute-start.5) | collective-permute-done | bytes 36896 | tf_op jit(solution)/shard_map/ppermute | solution.py:168
  47.6 5.9 %stencil.1 = (f32[3,8,8,128]{3,2,1,0:T(8,128)}, f32[3,4,4,128]{3,2,1,0:T(4,128)S(1)}) custom-call(s32[1]{0:T(128)} %bitcast.gy_ref, f32[3,8,8,128]{3,2,1,0:T(8,128)S(1)} %broadcast_select_fusion.v_ref, f32[3,8,8,128]{3,2,1,0:T(8,128)S(1)} %collective-permute-done.zl_ref, f32[3,8,8,128]{3,2,1,0:T(8,128)S(1)} %collective-permute-done.1.zh_ref, ...), custom_call_target="tpu_custom_call" | custom-call | tf_op jit(solution)/shard_map/stencil/pallas_call | solution.py:195
  53.5 0.0 copy-done
  53.6 0.6 fusion
  54.1 13.1 %all_to_all.15 = f32[32,4,128]{2,1,0:T(4,128)S(1)} all-to-all(f32[32,4,128]{2,1,0:T(4,128)S(1)} %bitcast.5), channel_id=1, replica_groups={{0,1,2,3,4,5,6,7,8,9,10,11,12,13,14,15,16,17,18,19,20,21,22,23,24,25,26..., dimensions={0} | all-to-all | bytes 131072 | tf_op jit(solution)/shard_map/all_to_all | solution.py:206
  67.3 18.7 %all_to_all.16 = f32[32,4,128]{2,1,0:T(4,128)S(1)} all-to-all(f32[32,4,128]{2,1,0:T(4,128)S(1)} %broadcast_in_dim.9), channel_id=1, replica_groups={{0,32,64,96,128,160,192,224,256,288,320,352,384,416,448,480,512,544,576..., dimensions={0} | all-to-all | bytes 131072 | tf_op jit(solution)/shard_map/all_to_all | solution.py:206
  86.1 13.2 %all_to_all.17 = f32[32,4,128]{2,1,0:T(4,128)S(1)} all-to-all(f32[32,4,128]{2,1,0:T(4,128)S(1)} %broadcast_in_dim.10), channel_id=1, replica_groups={{0,1,2,3,4,5,6,7,8,9,10,11,12,13,14,15,16,17,18,19,20,21,22,23,24,25,26..., dimensions={0} | all-to-all | bytes 131072 | tf_op jit(solution)/shard_map/all_to_all | solution.py:206
  99.2 4.1 %iterate.1 = (f32[128,128]{1,0:T(8,128)}, bf16[128,128]{1,0:T(8,128)(2,1)S(1)}) custom-call(f32[128,128]{1,0:T(8,128)S(1)} %bitcast.4), custom_call_target="tpu_custom_call" | custom-call | tf_op jit(solution)/shard_map/iterate/pallas_call | solution.py:256
  103.3 0.6 convolution_convert_fusion
  103.9 2.0 %reshape.45 = bf16[128,3,4,4,128]{4,3,2,1,0:T(4,128)(2,1)} reshape(bf16[128,6144]{1,0:T(8,128)(2,1)S(1)} %convolution_convert_fusion) | data formatting | bytes 3145728 | tf_op jit(solution)/shard_map/reshape | solution.py:267
  (7 shorter events, 0.2 us)
Async XLA Ops:
  0.6 10.9 %collective-permute-start.1 = (f32[3,8,8,128]{3,2,1,0:T(8,128)}, f32[3,8,8,128]{3,2,1,0:T(8,128)S(1)}, u32[]{:S(2)}, u32[]{:S(2)}) collective-permute-start(f32[3,8,8,128]{3,2,1,0:T(8,128)} %param.4), channel_id=1, source_target_pairs={{0,15},{1,0},{2,1},{3,2},{4,3},{5,4},{6,5},{7,6},{8,7},{9,8},{10,9... | collective-permute-start | bytes 294920 | tf_op jit(solution)/shard_map/ppermute | solution.py:168
  8.7 7.7 %collective-permute-start = (f32[3,8,8,128]{3,2,1,0:T(8,128)}, f32[3,8,8,128]{3,2,1,0:T(8,128)S(1)}, u32[]{:S(2)}, u32[]{:S(2)}) collective-permute-start(f32[3,8,8,128]{3,2,1,0:T(8,128)} %param.4), channel_id=1, source_target_pairs={{0,1},{1,2},{2,3},{3,4},{4,5},{5,6},{6,7},{7,8},{8,9},{9,10},{10,1... | collective-permute-start | bytes 294920 | tf_op jit(solution)/shard_map/ppermute | solution.py:168
  16.4 26.4 %copy-start.2 = (f32[64]{0:T(128)S(1)}, f32[64]{0:T(128)}, u32[]{:S(2)}) copy-start(f32[64]{0:T(128)} %param.6) | copy-start | bytes 772
  16.4 10.9 %collective-permute-start.2 = (f32[3,6,24,128]{3,2,1,0:T(8,128)S(1)}, f32[3,6,24,128]{3,2,1,0:T(8,128)S(1)}, u32[]{:S(2)}, u32[]{:S(2)}) collective-permute-start(f32[3,6,24,128]{3,2,1,0:T(8,128)S(1)} %get-tuple-element.11), channel_id=1, source_target_pairs={{0,16},{16,32},{32,48},{48,64},{64,80},{80,96},{96,112},{112,128},... | collective-permute-start | bytes 663560 | tf_op jit(solution)/shard_map/ppermute | solution.py:168
  19.8 7.5 %collective-permute-start.3 = (f32[3,6,24,128]{3,2,1,0:T(8,128)S(1)}, f32[3,6,24,128]{3,2,1,0:T(8,128)S(1)}, u32[]{:S(2)}, u32[]{:S(2)}) collective-permute-start(f32[3,6,24,128]{3,2,1,0:T(8,128)S(1)} %get-tuple-element.12), channel_id=1, source_target_pairs={{0,240},{16,0},{32,16},{48,32},{64,48},{80,64},{96,80},{112,96},{1... | collective-permute-start | bytes 663560 | tf_op jit(solution)/shard_map/ppermute | solution.py:168
  27.2 16.6 %copy-start.1 = (bf16[63,3,4,4,128]{4,3,2,1,0:T(4,128)(2,1)S(1)}, bf16[63,3,4,4,128]{4,3,2,1,0:T(4,128)(2,1)}, u32[]{:S(2)}) copy-start(bf16[63,3,4,4,128]{4,3,2,1,0:T(4,128)(2,1)} %param.7) | copy-start | bytes 2322436
  27.7 16.6 %collective-permute-start.4 = (f32[9,8,128]{2,1,0:T(8,128)S(1)}, f32[9,8,128]{2,1,0:T(8,128)S(1)}, u32[]{:S(2)}, u32[]{:S(2)}) collective-permute-start(f32[9,8,128]{2,1,0:T(8,128)S(1)} %get-tuple-element.13), channel_id=1, source_target_pairs={{0,768},{256,0},{512,256},{768,512},{1,769},{257,1},{513,257},{769... | collective-permute-start | bytes 110600 | tf_op jit(solution)/shard_map/ppermute | solution.py:168
  40.8 6.8 %collective-permute-start.5 = (f32[9,8,128]{2,1,0:T(8,128)S(1)}, f32[9,8,128]{2,1,0:T(8,128)S(1)}, u32[]{:S(2)}, u32[]{:S(2)}) collective-permute-start(f32[9,8,128]{2,1,0:T(8,128)S(1)} %get-tuple-element.14), channel_id=1, source_target_pairs={{0,256},{256,512},{512,768},{768,0},{1,257},{257,513},{513,769},{7... | collective-permute-start | bytes 110600 | tf_op jit(solution)/shard_map/ppermute | solution.py:168
  43.8 9.7 %copy-start = (bf16[64,6144]{1,0:T(8,128)(2,1)S(1)}, bf16[64,6144]{1,0:T(8,128)(2,1)}, u32[]{:S(2)}) copy-start(bf16[64,6144]{1,0:T(8,128)(2,1)} %multiply_convert_fusion) | copy-start | bytes 2359300

commit v6 on v5

--- a/solution.py
+++ b/solution.py
@@ -134,8 +134,7 @@
         plane(depth + 1, 2, 1)
         plane(PLANES - 2 - depth, 2, 1)
 
-        @pl.loop(depth + 2, PLANES - 2 - depth, unroll=2)
-        def _(y):
+        for y in range(depth + 2, PLANES - 2 - depth):
             plane(y, 2, 2)
 
         close(target)

time: 106 us -> 105 us (level)
  Pallas kernels: 10.5 us -> 9.31 us
    pallas_call x1, Pallas kernels: 5.88 us -> 4.72 us  [advance(): pl.pallas_call(functools.partial(_stencil_kernel, last=lax.axis_size('gy'...]
where the time goes in v6:
time: 105 us
  blocking collectives  45 us (43%)
  starting transfers between devices  34.2 us (33%)
  Pallas kernels  9.31 us (9%)
  waiting for transfers between devices  8.2 us (8%)
  local copies, waits for them, and re-layouts  4.18 us (4%)
  other arithmetic  2.04 us (2%)
  matrix products  1.13 us (1%)
    all_to_all x3, blocking collectives, exchanged(): return lax.all_to_all(blocks, axes, 0, 0, axis_index_groups=groups)  45 us
    ppermute x6, starting transfers between devices, shift(): return lax.ppermute(x, axis, [(i, (i + step) % n) for i in range(n)])  34.2 us
    ppermute x6, waiting for transfers between devices, shift(): return lax.ppermute(x, axis, [(i, (i + step) % n) for i in range(n)])  8.2 us
    pallas_call x1, Pallas kernels, advance(): pl.pallas_call(functools.partial(_stencil_kernel, last=lax.axis_size('gy'...  4.72 us
    pallas_call x1, Pallas kernels, local(): pl.pallas_call(functools.partial(_iterate_kernel, total_rows=total_rows),...  4.12 us
  transfers between devices with their start and end apart: 6, of which 2 were waited for; matrix products, arithmetic and copies ran while one was open for 4% of the time, Pallas kernels for 0%

profile of v6, /device:TPU:1, one launch (start us, length us, event | category | flops | bytes accessed | tf_op | source)
XLA Modules:
  0.0 104.8 jit_solution(12896108823702093053)
XLA Ops:
  0.6 8.0 %collective-permute-start.1 = (f32[3,8,8,128]{3,2,1,0:T(8,128)}, f32[3,8,8,128]{3,2,1,0:T(8,128)S(1)}, u32[]{:S(2)}, u32[]{:S(2)}) collective-permute-start(f32[3,8,8,128]{3,2,1,0:T(8,128)} %param.4), channel_id=1, source_target_pairs={{0,15},{1,0},{2,1},{3,2},{4,3},{5,4},{6,5},{7,6},{8,7},{9,8},{10,9... | collective-permute-start | bytes 294920 | tf_op jit(solution)/shard_map/ppermute | solution.py:167
  8.7 1.9 %collective-permute-start = (f32[3,8,8,128]{3,2,1,0:T(8,128)}, f32[3,8,8,128]{3,2,1,0:T(8,128)S(1)}, u32[]{:S(2)}, u32[]{:S(2)}) collective-permute-start(f32[3,8,8,128]{3,2,1,0:T(8,128)} %param.4), channel_id=1, source_target_pairs={{0,1},{1,2},{2,3},{3,4},{4,5},{5,6},{6,7},{7,8},{8,9},{9,10},{10,1... | collective-permute-start | bytes 294920 | tf_op jit(solution)/shard_map/ppermute | solution.py:167
  10.6 0.9 broadcast_select_fusion.v_ref
  11.5 0.0 collective-permute-done.1.zh_ref
  11.5 4.8 %collective-permute-done.zl_ref = f32[3,8,8,128]{3,2,1,0:T(8,128)S(1)} collective-permute-done((f32[3,8,8,128]{3,2,1,0:T(8,128)}, f32[3,8,8,128]{3,2,1,0:T(8,128)S(1)}, u32[]{:S(2)}, u32[]{:S(2)}) %collective-permute-start) | collective-permute-done | bytes 98336 | tf_op jit(solution)/shard_map/ppermute | solution.py:167
  16.4 0.0 copy-start.2
  16.4 3.4 %collective-permute-start.2 = (f32[3,6,24,128]{3,2,1,0:T(8,128)S(1)}, f32[3,6,24,128]{3,2,1,0:T(8,128)S(1)}, u32[]{:S(2)}, u32[]{:S(2)}) collective-permute-start(f32[3,6,24,128]{3,2,1,0:T(8,128)S(1)} %get-tuple-element.11), channel_id=1, source_target_pairs={{0,16},{16,32},{32,48},{48,64},{64,80},{80,96},{96,112},{112,128},... | collective-permute-start | bytes 663560 | tf_op jit(solution)/shard_map/ppermute | solution.py:167
  19.8 5.8 %collective-permute-start.3 = (f32[3,6,24,128]{3,2,1,0:T(8,128)S(1)}, f32[3,6,24,128]{3,2,1,0:T(8,128)S(1)}, u32[]{:S(2)}, u32[]{:S(2)}) collective-permute-start(f32[3,6,24,128]{3,2,1,0:T(8,128)S(1)} %get-tuple-element.12), channel_id=1, source_target_pairs={{0,240},{16,0},{32,16},{48,32},{64,48},{80,64},{96,80},{112,96},{1... | collective-permute-start | bytes 663560 | tf_op jit(solution)/shard_map/ppermute | solution.py:167
  25.6 1.6 %reshape.46 = f32[64,6144]{1,0:T(8,128)S(1)} reshape(bf16[64,3,4,4,128]{4,3,2,1,0:T(4,128)(2,1)} %param.5) | data formatting | bytes 2359296 | tf_op jit(solution)/shard_map/convert_element_type | solution.py:248
  27.2 0.0 copy-start.1
  27.3 0.0 collective-permute-done.2.yl_ref
  27.3 0.0 collective-permute-done.3.yh_ref
  27.3 0.4 faces_x.1
  27.7 13.1 %collective-permute-start.4 = (f32[9,8,128]{2,1,0:T(8,128)S(1)}, f32[9,8,128]{2,1,0:T(8,128)S(1)}, u32[]{:S(2)}, u32[]{:S(2)}) collective-permute-start(f32[9,8,128]{2,1,0:T(8,128)S(1)} %get-tuple-element.13), channel_id=1, source_target_pairs={{0,768},{256,0},{512,256},{768,512},{1,769},{257,1},{513,257},{769... | collective-permute-start | bytes 110600 | tf_op jit(solution)/shard_map/ppermute | solution.py:167
  40.8 1.9 %collective-permute-start.5 = (f32[9,8,128]{2,1,0:T(8,128)S(1)}, f32[9,8,128]{2,1,0:T(8,128)S(1)}, u32[]{:S(2)}, u32[]{:S(2)}) collective-permute-start(f32[9,8,128]{2,1,0:T(8,128)S(1)} %get-tuple-element.14), channel_id=1, source_target_pairs={{0,256},{256,512},{512,768},{768,0},{1,257},{257,513},{513,769},{7... | collective-permute-start | bytes 110600 | tf_op jit(solution)/shard_map/ppermute | solution.py:167
  42.8 0.0 copy-done.2
  42.8 1.0 multiply_convert_fusion
  43.8 0.0 copy-done.1
  43.8 0.0 copy-start
  43.8 0.5 reshape.42
  44.3 0.0 collective-permute-done.4.xh_ref
  44.3 3.4 %collective-permute-done.5.xl_ref = f32[9,8,128]{2,1,0:T(8,128)S(1)} collective-permute-done((f32[9,8,128]{2,1,0:T(8,128)S(1)}, f32[9,8,128]{2,1,0:T(8,128)S(1)}, u32[]{:S(2)}, u32[]{:S(2)}) %collective-permute-start.5) | collective-permute-done | bytes 36896 | tf_op jit(solution)/shard_map/ppermute | solution.py:167
  47.6 4.7 %stencil.1 = (f32[3,8,8,128]{3,2,1,0:T(8,128)}, f32[3,4,4,128]{3,2,1,0:T(4,128)S(1)}) custom-call(s32[1]{0:T(128)} %bitcast.gy_ref, f32[3,8,8,128]{3,2,1,0:T(8,128)S(1)} %broadcast_select_fusion.v_ref, f32[3,8,8,128]{3,2,1,0:T(8,128)S(1)} %collective-permute-done.zl_ref, f32[3,8,8,128]{3,2,1,0:T(8,128)S(1)} %collective-permute-done.1.zh_ref, ...), custom_call_target="tpu_custom_call" | custom-call | tf_op jit(solution)/shard_map/stencil/pallas_call | solution.py:194
  52.4 0.0 copy-done
  52.4 0.6 fusion
  53.0 13.1 %all_to_all.15 = f32[32,4,128]{2,1,0:T(4,128)S(1)} all-to-all(f32[32,4,128]{2,1,0:T(4,128)S(1)} %bitcast.5), channel_id=1, replica_groups={{0,1,2,3,4,5,6,7,8,9,10,11,12,13,14,15,16,17,18,19,20,21,22,23,24,25,26..., dimensions={0} | all-to-all | bytes 131072 | tf_op jit(solution)/shard_map/all_to_all | solution.py:205
  66.1 18.7 %all_to_all.16 = f32[32,4,128]{2,1,0:T(4,128)S(1)} all-to-all(f32[32,4,128]{2,1,0:T(4,128)S(1)} %broadcast_in_dim.9), channel_id=1, replica_groups={{0,32,64,96,128,160,192,224,256,288,320,352,384,416,448,480,512,544,576..., dimensions={0} | all-to-all | bytes 131072 | tf_op jit(solution)/shard_map/all_to_all | solution.py:205
  84.9 13.2 %all_to_all.17 = f32[32,4,128]{2,1,0:T(4,128)S(1)} all-to-all(f32[32,4,128]{2,1,0:T(4,128)S(1)} %broadcast_in_dim.10), channel_id=1, replica_groups={{0,1,2,3,4,5,6,7,8,9,10,11,12,13,14,15,16,17,18,19,20,21,22,23,24,25,26..., dimensions={0} | all-to-all | bytes 131072 | tf_op jit(solution)/shard_map/all_to_all | solution.py:205
  98.1 4.1 %iterate.1 = (f32[128,128]{1,0:T(8,128)}, bf16[128,128]{1,0:T(8,128)(2,1)S(1)}) custom-call(f32[128,128]{1,0:T(8,128)S(1)} %bitcast.4), custom_call_target="tpu_custom_call" | custom-call | tf_op jit(solution)/shard_map/iterate/pallas_call | solution.py:255
  102.2 0.6 convolution_convert_fusion
  102.7 2.0 %reshape.45 = bf16[128,3,4,4,128]{4,3,2,1,0:T(4,128)(2,1)} reshape(bf16[128,6144]{1,0:T(8,128)(2,1)S(1)} %convolution_convert_fusion) | data formatting | bytes 3145728 | tf_op jit(solution)/shard_map/reshape | solution.py:266
  (7 shorter events, 0.2 us)
Async XLA Ops:
  0.6 10.9 %collective-permute-start.1 = (f32[3,8,8,128]{3,2,1,0:T(8,128)}, f32[3,8,8,128]{3,2,1,0:T(8,128)S(1)}, u32[]{:S(2)}, u32[]{:S(2)}) collective-permute-start(f32[3,8,8,128]{3,2,1,0:T(8,128)} %param.4), channel_id=1, source_target_pairs={{0,15},{1,0},{2,1},{3,2},{4,3},{5,4},{6,5},{7,6},{8,7},{9,8},{10,9... | collective-permute-start | bytes 294920 | tf_op jit(solution)/shard_map/ppermute | solution.py:167
  8.7 7.7 %collective-permute-start = (f32[3,8,8,128]{3,2,1,0:T(8,128)}, f32[3,8,8,128]{3,2,1,0:T(8,128)S(1)}, u32[]{:S(2)}, u32[]{:S(2)}) collective-permute-start(f32[3,8,8,128]{3,2,1,0:T(8,128)} %param.4), channel_id=1, source_target_pairs={{0,1},{1,2},{2,3},{3,4},{4,5},{5,6},{6,7},{7,8},{8,9},{9,10},{10,1... | collective-permute-start | bytes 294920 | tf_op jit(solution)/shard_map/ppermute | solution.py:167
  16.4 26.4 %copy-start.2 = (f32[64]{0:T(128)S(1)}, f32[64]{0:T(128)}, u32[]{:S(2)}) copy-start(f32[64]{0:T(128)} %param.6) | copy-start | bytes 772
  16.4 10.9 %collective-permute-start.2 = (f32[3,6,24,128]{3,2,1,0:T(8,128)S(1)}, f32[3,6,24,128]{3,2,1,0:T(8,128)S(1)}, u32[]{:S(2)}, u32[]{:S(2)}) collective-permute-start(f32[3,6,24,128]{3,2,1,0:T(8,128)S(1)} %get-tuple-element.11), channel_id=1, source_target_pairs={{0,16},{16,32},{32,48},{48,64},{64,80},{80,96},{96,112},{112,128},... | collective-permute-start | bytes 663560 | tf_op jit(solution)/shard_map/ppermute | solution.py:167
  19.8 7.5 %collective-permute-start.3 = (f32[3,6,24,128]{3,2,1,0:T(8,128)S(1)}, f32[3,6,24,128]{3,2,1,0:T(8,128)S(1)}, u32[]{:S(2)}, u32[]{:S(2)}) collective-permute-start(f32[3,6,24,128]{3,2,1,0:T(8,128)S(1)} %get-tuple-element.12), channel_id=1, source_target_pairs={{0,240},{16,0},{32,16},{48,32},{64,48},{80,64},{96,80},{112,96},{1... | collective-permute-start | bytes 663560 | tf_op jit(solution)/shard_map/ppermute | solution.py:167
  27.2 16.6 %copy-start.1 = (bf16[63,3,4,4,128]{4,3,2,1,0:T(4,128)(2,1)S(1)}, bf16[63,3,4,4,128]{4,3,2,1,0:T(4,128)(2,1)}, u32[]{:S(2)}) copy-start(bf16[63,3,4,4,128]{4,3,2,1,0:T(4,128)(2,1)} %param.7) | copy-start | bytes 2322436
  27.7 16.6 %collective-permute-start.4 = (f32[9,8,128]{2,1,0:T(8,128)S(1)}, f32[9,8,128]{2,1,0:T(8,128)S(1)}, u32[]{:S(2)}, u32[]{:S(2)}) collective-permute-start(f32[9,8,128]{2,1,0:T(8,128)S(1)} %get-tuple-element.13), channel_id=1, source_target_pairs={{0,768},{256,0},{512,256},{768,512},{1,769},{257,1},{513,257},{769... | collective-permute-start | bytes 110600 | tf_op jit(solution)/shard_map/ppermute | solution.py:167
  40.8 6.8 %collective-permute-start.5 = (f32[9,8,128]{2,1,0:T(8,128)S(1)}, f32[9,8,128]{2,1,0:T(8,128)S(1)}, u32[]{:S(2)}, u32[]{:S(2)}) collective-permute-start(f32[9,8,128]{2,1,0:T(8,128)S(1)} %get-tuple-element.14), channel_id=1, source_target_pairs={{0,256},{256,512},{512,768},{768,0},{1,257},{257,513},{513,769},{7... | collective-permute-start | bytes 110600 | tf_op jit(solution)/shard_map/ppermute | solution.py:167
  43.8 8.6 %copy-start = (bf16[64,6144]{1,0:T(8,128)(2,1)S(1)}, bf16[64,6144]{1,0:T(8,128)(2,1)}, u32[]{:S(2)}) copy-start(bf16[64,6144]{1,0:T(8,128)(2,1)} %multiply_convert_fusion) | copy-start | bytes 2359300
